TPU v7x, 32 devices: a whole 2x2x4 slice. The times are simulated.
32 devices in a mesh: rep: 4 (over x, core), fsdp: 8 (over z, y).
Axes of the slice: x: 2, y: 2, z: 4, core: 2. Of those that a mesh axis runs over, the one named last changes fastest.
Arguments:
- sequence_entries: bfloat16 [160, 96, 768], P(('rep', 'fsdp')), may hold values from -6 to 6
- picture_descriptors: bfloat16 [160, 257, 1408], P(('rep', 'fsdp')), may hold values from -6 to 6
- sentence_numbering: int32 [160, 64], P(('rep', 'fsdp')), may hold values from 0 to 1, never falling along the last dimension, each value on 1 to 48 neighbouring positions
- sentence_picture_owner: int32 [320], P(('rep', 'fsdp')), may hold values from 0 to 159
- upstream_adjoint: bfloat16 [160, 96, 768], P(('rep', 'fsdp')), may hold values from -6 to 6
- attend_triple_matrix: bfloat16 [768, 2304], P('fsdp'), may hold values from -0.21875 to 0.21875
- inward_result_matrix: bfloat16 [768, 768], P('fsdp'), may hold values from -1.25 to 1.25
- inward_result_offset: bfloat16 [768], P('fsdp'), may hold values from -2 to 2
- inward_center_scale: bfloat16 [768], P('fsdp'), may hold values from 0.5 to 1.5
- inward_center_shift: bfloat16 [768], P('fsdp'), may hold values from -1 to 1
- mixing_asker_matrix: bfloat16 [768, 768], P('fsdp'), may hold values from -0.21875 to 0.21875
- visual_lookup_pairs: bfloat16 [1408, 1536], P('fsdp'), may hold values from -0.15625 to 0.15625
- mixing_result_matrix: bfloat16 [768, 768], P('fsdp'), may hold values from -3.5 to 3.5
- mixing_result_offset: bfloat16 [768], P('fsdp'), may hold values from -2 to 2
- mixing_center_scale: bfloat16 [768], P('fsdp'), may hold values from 0.5 to 1.5
- mixing_center_shift: bfloat16 [768], P('fsdp'), may hold values from -1 to 1
- widening_matrix: bfloat16 [768, 3072], P('fsdp'), may hold values from -0.21875 to 0.21875
- widening_offset: bfloat16 [3072], P('fsdp'), may hold values from -2.5 to 2.5
- narrowing_matrix: bfloat16 [3072, 768], P('fsdp'), may hold values from -0.109375 to 0.109375
- narrowing_offset: bfloat16 [768], P('fsdp'), may hold values from -2 to 2
- perceptron_center_scale: bfloat16 [768], P('fsdp'), may hold values from 0.5 to 1.5
- perceptron_center_shift: bfloat16 [768], P('fsdp'), may hold values from -1 to 1
- picture_mapping_matrix: bfloat16 [768, 256], P('fsdp'), may hold values from -0.21875 to 0.21875
- picture_vector_offset: bfloat16 [256], P('fsdp'), may hold values from -0.5 to 0.5
- sentence_mapping_matrix: bfloat16 [768, 256], P('fsdp'), may hold values from -0.21875 to 0.21875
- sentence_vector_offset: bfloat16 [256], P('fsdp'), may hold values from -1.5 to 1.5
- logit_sharpness: float32 [], replicated, may hold values from 0.025 to 0.05
Outputs:
- out: bfloat16 [160, 96, 768], P(('rep', 'fsdp'))
- incoming_sequence_adjoint: float32 [160, 96, 768], P(('rep', 'fsdp'))
- qkv_weight_grad: float32 [768, 2304], P('fsdp')
- self_out_grad: float32 [768, 768], P('fsdp')
- self_bias_grad: float32 [768], P('fsdp')
- self_gain_grad: float32 [768], P('fsdp')
- self_shift_grad: float32 [768], P('fsdp')
- cross_query_grad: float32 [768, 768], P('fsdp')
- cross_keyval_grad: float32 [1408, 1536], P('fsdp')
- cross_out_grad: float32 [768, 768], P('fsdp')
- cross_bias_grad: float32 [768], P('fsdp')
- cross_gain_grad: float32 [768], P('fsdp')
- cross_shift_grad: float32 [768], P('fsdp')
- up_weight_grad: float32 [768, 3072], P('fsdp')
- up_bias_grad: float32 [3072], P('fsdp')
- down_weight_grad: float32 [3072, 768], P('fsdp')
- down_bias_grad: float32 [768], P('fsdp')
- feed_gain_grad: float32 [768], P('fsdp')
- feed_shift_grad: float32 [768], P('fsdp')
- image_proj_grad: float32 [768, 256], P('fsdp')
- image_bias_grad: float32 [256], P('fsdp')
- text_proj_grad: float32 [768, 256], P('fsdp')
- text_bias_grad: float32 [256], P('fsdp')
- sharpness_adjoint: float32 [], replicated
Inputs may be any that keep to these rules, and one draw needn't show every extreme that they name: `sentence_numbering`: in each row the caption numbers never fall and each of the 2 captions has 16 to 48 tokens.
All inputs are finite; a program needn't handle non-finite values.
Results may differ from a plain program's by a relative error of at most 0.02.
Values may be sent and summed in bfloat16 or wider, within the bound.
No kernel may reach another device: no remote copies, remote signals or barrier semaphores. Data moves between devices by JAX's collectives and lax.ppermute only.
A program may use at most 192 MiB of HBM per device.

v0:
```python
from functools import partial

import jax
import jax.numpy as jnp
from jax import lax
from jax.sharding import PartitionSpec as P

HEADS = 12
HEAD = 64
QUERY = 32
CAPS_ROW = 2


def project(values, matrix):
    return jnp.einsum("...d,df->...f", values, matrix, preferred_element_type=jnp.float32)


def project_back(gradient, matrix):
    return jnp.einsum("...f,df->...d", gradient, matrix, preferred_element_type=jnp.float32)


def outer_sum(values, gradient):
    flat_values = values.reshape(-1, values.shape[-1])
    flat_gradient = gradient.reshape(-1, gradient.shape[-1])
    return lax.dot_general(
        flat_values, flat_gradient, (((0,), (0,)), ((), ())), preferred_element_type=jnp.float32
    )


def column_sum(gradient):
    return jnp.sum(gradient.reshape(-1, gradient.shape[-1]), axis=0, dtype=jnp.float32)


def layer_norm(summed, norm_gain, norm_shift):
    center = summed - jnp.mean(summed, axis=-1, keepdims=True)
    spread = jnp.mean(center * center, axis=-1, keepdims=True)
    return center * lax.rsqrt(spread + 1e-06) * norm_gain + norm_shift


def norm_back(summed, norm_gain, norm_shift, gradient):
    _, reverse_sweep_rule = jax.vjp(layer_norm, summed, norm_gain, norm_shift)
    return reverse_sweep_rule(gradient)


def unit_rows(values):
    return values * lax.rsqrt(jnp.sum(values * values, axis=-1, keepdims=True) + 1e-06)


def exact_gelu(values):
    return jax.nn.gelu(values, approximate=False)


def token_kinds(sentence_numbering):
    query_kinds = jnp.zeros((sentence_numbering.shape[0], QUERY), jnp.int32)
    return jnp.concatenate([query_kinds, sentence_numbering + 1], axis=1)


def caption_picker(sentence_numbering):
    caption_ids = jnp.arange(CAPS_ROW, dtype=jnp.int32)
    starts = jnp.sum(
        (sentence_numbering[:, None, :] < caption_ids[None, :, None]).astype(jnp.int32), axis=2
    )
    places = jnp.arange(sentence_numbering.shape[1], dtype=jnp.int32)
    return (places[None, None, :] == starts[:, :, None]).astype(jnp.float32)


def split_heads(values):
    return values.reshape(values.shape[0], values.shape[1], HEADS, values.shape[2] // HEADS)


def scores_of(queries, key_rows, allowed):
    scaling = HEAD ** (-0.5)
    scores = (
        jnp.einsum(
            "bqhd,bkhd->bhqk",
            split_heads(queries),
            split_heads(key_rows),
            preferred_element_type=jnp.float32,
        )
        * scaling
    )
    if allowed is not None:
        scores = jnp.where(allowed[:, None], scores, -1e30)
    return (scores, scaling)


def attend(queries, key_rows, value_rows, allowed):
    scores, scaling = scores_of(queries, key_rows, allowed)
    highest = jnp.max(scores, axis=-1, keepdims=True)
    exponent = jnp.exp(scores - highest)
    normalizer = jnp.sum(exponent, axis=-1, keepdims=True)
    attention_probs = (exponent / normalizer).astype(jnp.bfloat16)
    mixed_heads = jnp.einsum(
        "bhqk,bkhd->bqhd",
        attention_probs,
        split_heads(value_rows),
        preferred_element_type=jnp.float32,
    )
    mixed_heads = mixed_heads.reshape(queries.shape[0], queries.shape[1], -1).astype(jnp.bfloat16)
    return (mixed_heads, highest + jnp.log(normalizer))


def attend_back(queries, key_rows, value_rows, allowed, log_total, grad_mixed):
    scores, scaling = scores_of(queries, key_rows, allowed)
    attention_probs = jnp.exp(scores - log_total)
    upstream = split_heads(grad_mixed)
    grad_value = jnp.einsum(
        "bhqk,bqhd->bkhd",
        attention_probs.astype(jnp.bfloat16),
        upstream,
        preferred_element_type=jnp.float32,
    )
    grad_probs = jnp.einsum(
        "bqhd,bkhd->bhqk", upstream, split_heads(value_rows), preferred_element_type=jnp.float32
    )
    grad_scores = attention_probs * (
        grad_probs - jnp.sum(attention_probs * grad_probs, axis=-1, keepdims=True)
    )
    grad_scores = grad_scores.astype(jnp.bfloat16)
    grad_query = (
        jnp.einsum(
            "bhqk,bkhd->bqhd",
            grad_scores,
            split_heads(key_rows),
            preferred_element_type=jnp.float32,
        )
        * scaling
    )
    grad_key = (
        jnp.einsum(
            "bhqk,bqhd->bkhd", grad_scores, split_heads(queries), preferred_element_type=jnp.float32
        )
        * scaling
    )
    batch = queries.shape[0]
    return (
        grad_query.reshape(batch, queries.shape[1], -1),
        grad_key.reshape(batch, key_rows.shape[1], -1),
        grad_value.reshape(batch, key_rows.shape[1], -1),
    )


def run_self(self_full, sequence_entries, allowed):
    (
        attend_triple_matrix,
        inward_result_matrix,
        inward_result_offset,
        inward_center_scale,
        inward_center_shift,
    ) = self_full
    model_width = sequence_entries.shape[-1]
    qkv_rows = project(sequence_entries, attend_triple_matrix).astype(jnp.bfloat16)
    mixed_heads, log_total = attend(
        qkv_rows[..., :model_width],
        qkv_rows[..., model_width : 2 * model_width],
        qkv_rows[..., 2 * model_width :],
        allowed,
    )
    summed = (
        sequence_entries.astype(jnp.float32)
        + project(mixed_heads, inward_result_matrix)
        + inward_result_offset.astype(jnp.float32)
    )
    inner_rows = layer_norm(
        summed, inward_center_scale.astype(jnp.float32), inward_center_shift.astype(jnp.float32)
    )
    return (inner_rows, (qkv_rows, log_total, mixed_heads, summed))


def run_cross(cross_full, inner_rows, picture_descriptors):
    (
        mixing_asker_matrix,
        visual_lookup_pairs,
        mixing_result_matrix,
        mixing_result_offset,
        mixing_center_scale,
        mixing_center_shift,
    ) = cross_full
    model_width = inner_rows.shape[-1]
    head_rows = inner_rows[:, :QUERY]
    low_rows = head_rows.astype(jnp.bfloat16)
    asked_rows = project(low_rows, mixing_asker_matrix).astype(jnp.bfloat16)
    keyval = project(picture_descriptors, visual_lookup_pairs).astype(jnp.bfloat16)
    seen_rows, log_total = attend(
        asked_rows, keyval[..., :model_width], keyval[..., model_width:], None
    )
    summed = (
        head_rows
        + project(seen_rows, mixing_result_matrix)
        + mixing_result_offset.astype(jnp.float32)
    )
    normed = layer_norm(
        summed, mixing_center_scale.astype(jnp.float32), mixing_center_shift.astype(jnp.float32)
    )
    merged = jnp.concatenate([normed, inner_rows[:, QUERY:]], axis=1)
    return (merged, (low_rows, asked_rows, keyval, log_total, seen_rows, summed))


def run_feed(feed_full, merged):
    (
        widening_matrix,
        widening_offset,
        narrowing_matrix,
        narrowing_offset,
        perceptron_center_scale,
        perceptron_center_shift,
    ) = feed_full
    low_rows = merged.astype(jnp.bfloat16)
    pre_act = project(low_rows, widening_matrix) + widening_offset.astype(jnp.float32)
    activated = exact_gelu(pre_act).astype(jnp.bfloat16)
    summed = merged + project(activated, narrowing_matrix) + narrowing_offset.astype(jnp.float32)
    finishing_lines = layer_norm(
        summed,
        perceptron_center_scale.astype(jnp.float32),
        perceptron_center_shift.astype(jnp.float32),
    )
    return (finishing_lines, (low_rows, pre_act, activated, summed))


def feed_back(feed_full, kept_state, grad_final):
    (
        widening_matrix,
        widening_offset,
        narrowing_matrix,
        narrowing_offset,
        perceptron_center_scale,
        perceptron_center_shift,
    ) = feed_full
    low_rows, pre_act, activated, summed = kept_state
    grad_sum, grad_gain, grad_shift = norm_back(
        summed,
        perceptron_center_scale.astype(jnp.float32),
        perceptron_center_shift.astype(jnp.float32),
        grad_final,
    )
    grad_third = grad_sum.astype(jnp.bfloat16)
    grad_active = project_back(grad_third, narrowing_matrix)
    _, gelu_pull = jax.vjp(exact_gelu, pre_act)
    grad_pre = gelu_pull(grad_active)[0].astype(jnp.bfloat16)
    grad_merged = grad_sum + project_back(grad_pre, widening_matrix)
    partials = (
        outer_sum(low_rows, grad_pre),
        column_sum(grad_pre),
        outer_sum(activated, grad_third),
        column_sum(grad_third),
        grad_gain,
        grad_shift,
    )
    return (grad_merged, partials)


def cross_back(cross_full, kept_state, picture_descriptors, grad_merged):
    (
        mixing_asker_matrix,
        visual_lookup_pairs,
        mixing_result_matrix,
        mixing_result_offset,
        mixing_center_scale,
        mixing_center_shift,
    ) = cross_full
    low_rows, asked_rows, keyval, log_total, seen_rows, summed = kept_state
    model_width = asked_rows.shape[-1]
    grad_sum, grad_gain, grad_shift = norm_back(
        summed,
        mixing_center_scale.astype(jnp.float32),
        mixing_center_shift.astype(jnp.float32),
        grad_merged[:, :QUERY],
    )
    grad_second = grad_sum.astype(jnp.bfloat16)
    grad_seen = project_back(grad_second, mixing_result_matrix).astype(jnp.bfloat16)
    grad_asked, grad_key, grad_value = attend_back(
        asked_rows, keyval[..., :model_width], keyval[..., model_width:], None, log_total, grad_seen
    )
    grad_asked = grad_asked.astype(jnp.bfloat16)
    grad_keyval = jnp.concatenate([grad_key, grad_value], axis=-1).astype(jnp.bfloat16)
    grad_head = grad_sum + project_back(grad_asked, mixing_asker_matrix)
    grad_inner = jnp.concatenate([grad_head, grad_merged[:, QUERY:]], axis=1)
    partials = (
        outer_sum(low_rows, grad_asked),
        outer_sum(picture_descriptors, grad_keyval),
        outer_sum(seen_rows, grad_second),
        column_sum(grad_second),
        grad_gain,
        grad_shift,
    )
    return (grad_inner, partials)


def self_back(self_full, kept_state, sequence_entries, allowed, grad_inner):
    (
        attend_triple_matrix,
        inward_result_matrix,
        inward_result_offset,
        inward_center_scale,
        inward_center_shift,
    ) = self_full
    qkv_rows, log_total, mixed_heads, summed = kept_state
    model_width = sequence_entries.shape[-1]
    grad_sum, grad_gain, grad_shift = norm_back(
        summed,
        inward_center_scale.astype(jnp.float32),
        inward_center_shift.astype(jnp.float32),
        grad_inner,
    )
    grad_first = grad_sum.astype(jnp.bfloat16)
    grad_mixed = project_back(grad_first, inward_result_matrix).astype(jnp.bfloat16)
    grad_query, grad_key, grad_value = attend_back(
        qkv_rows[..., :model_width],
        qkv_rows[..., model_width : 2 * model_width],
        qkv_rows[..., 2 * model_width :],
        allowed,
        log_total,
        grad_mixed,
    )
    grad_qkv = jnp.concatenate([grad_query, grad_key, grad_value], axis=-1).astype(jnp.bfloat16)
    incoming_sequence_adjoint = grad_sum + project_back(grad_qkv, attend_triple_matrix)
    partials = (
        outer_sum(sequence_entries, grad_qkv),
        outer_sum(mixed_heads, grad_first),
        column_sum(grad_first),
        grad_gain,
        grad_shift,
    )
    return (incoming_sequence_adjoint, partials)


def contrast(similar, reverse_sims, temper, positive, caption_total):
    image_side = jax.nn.logsumexp(similar / temper, axis=-1)
    text_side = jax.nn.logsumexp(reverse_sims / temper, axis=-1)
    matched = jnp.sum(similar * positive, axis=-1) / temper
    return jnp.sum(image_side + text_side - 2.0 * matched) / (2.0 * caption_total)


def on_device(
    sequence_entries,
    picture_descriptors,
    sentence_numbering,
    sentence_picture_owner,
    upstream_adjoint,
    attend_triple_matrix,
    inward_result_matrix,
    inward_result_offset,
    inward_center_scale,
    inward_center_shift,
    mixing_asker_matrix,
    visual_lookup_pairs,
    mixing_result_matrix,
    mixing_result_offset,
    mixing_center_scale,
    mixing_center_shift,
    widening_matrix,
    widening_offset,
    narrowing_matrix,
    narrowing_offset,
    perceptron_center_scale,
    perceptron_center_shift,
    picture_mapping_matrix,
    picture_vector_offset,
    sentence_mapping_matrix,
    sentence_vector_offset,
    logit_sharpness,
):
    segment_of = token_kinds(sentence_numbering)
    allowed = segment_of[:, :, None] == segment_of[:, None, :]
    picker = caption_picker(sentence_numbering)
    self_full = (
        lax.all_gather(attend_triple_matrix, "fsdp", axis=0, tiled=True),
        lax.all_gather(inward_result_matrix, "fsdp", axis=0, tiled=True),
        lax.all_gather(inward_result_offset, "fsdp", axis=0, tiled=True),
        lax.all_gather(inward_center_scale, "fsdp", axis=0, tiled=True),
        lax.all_gather(inward_center_shift, "fsdp", axis=0, tiled=True),
    )
    inner_rows, self_kept = run_self(self_full, sequence_entries, allowed)
    cross_full = (
        lax.all_gather(mixing_asker_matrix, "fsdp", axis=0, tiled=True),
        lax.all_gather(visual_lookup_pairs, "fsdp", axis=0, tiled=True),
        lax.all_gather(mixing_result_matrix, "fsdp", axis=0, tiled=True),
        lax.all_gather(mixing_result_offset, "fsdp", axis=0, tiled=True),
        lax.all_gather(mixing_center_scale, "fsdp", axis=0, tiled=True),
        lax.all_gather(mixing_center_shift, "fsdp", axis=0, tiled=True),
    )
    merged, cross_kept = run_cross(cross_full, inner_rows, picture_descriptors)
    feed_full = (
        lax.all_gather(widening_matrix, "fsdp", axis=0, tiled=True),
        lax.all_gather(widening_offset, "fsdp", axis=0, tiled=True),
        lax.all_gather(narrowing_matrix, "fsdp", axis=0, tiled=True),
        lax.all_gather(narrowing_offset, "fsdp", axis=0, tiled=True),
        lax.all_gather(perceptron_center_scale, "fsdp", axis=0, tiled=True),
        lax.all_gather(perceptron_center_shift, "fsdp", axis=0, tiled=True),
    )
    finishing_lines, feed_kept = run_feed(feed_full, merged)
    image_full, image_shift, text_full, text_shift = (
        lax.all_gather(picture_mapping_matrix, "fsdp", axis=0, tiled=True),
        lax.all_gather(picture_vector_offset, "fsdp", axis=0, tiled=True),
        lax.all_gather(sentence_mapping_matrix, "fsdp", axis=0, tiled=True),
        lax.all_gather(sentence_vector_offset, "fsdp", axis=0, tiled=True),
    )
    row_count = finishing_lines.shape[0]
    model_width = finishing_lines.shape[-1]
    pooled_low = jnp.mean(finishing_lines[:, :QUERY], axis=1).astype(jnp.bfloat16)
    image_raw = project(pooled_low, image_full) + image_shift.astype(jnp.float32)
    image_unit = unit_rows(image_raw).astype(jnp.bfloat16)
    captions = jnp.sum(picker[:, :, :, None] * finishing_lines[:, None, QUERY:, :], axis=2)
    caption_low = captions.reshape(-1, model_width).astype(jnp.bfloat16)
    text_raw = project(caption_low, text_full) + text_shift.astype(jnp.float32)
    text_unit = unit_rows(text_raw).astype(jnp.bfloat16)
    all_images, all_texts = (
        lax.all_gather(image_unit, ("rep", "fsdp"), axis=0, tiled=True),
        lax.all_gather(text_unit, ("rep", "fsdp"), axis=0, tiled=True),
    )
    image_ids = jnp.arange(all_images.shape[0], dtype=jnp.int32)
    positive = (sentence_picture_owner[:, None] == image_ids[None, :]).astype(jnp.float32)
    similar = lax.dot_general(
        text_unit, all_images, (((1,), (1,)), ((), ())), preferred_element_type=jnp.float32
    )
    chosen = jnp.dot(
        positive.astype(jnp.bfloat16), all_images, preferred_element_type=jnp.float32
    ).astype(jnp.bfloat16)
    reverse_sims = lax.dot_general(
        chosen, all_texts, (((1,), (1,)), ((), ())), preferred_element_type=jnp.float32
    )
    _, matching_reverse_rule = jax.vjp(
        partial(contrast, positive=positive, caption_total=all_texts.shape[0]),
        similar,
        reverse_sims,
        logit_sharpness,
    )
    adjoint_affinity, adjoint_flipped, sharpness_contribution = matching_reverse_rule(
        jnp.ones((), jnp.float32)
    )
    adjoint_affinity = adjoint_affinity.astype(jnp.bfloat16)
    adjoint_flipped = adjoint_flipped.astype(jnp.bfloat16)
    grad_text_here = jnp.dot(adjoint_affinity, all_images, preferred_element_type=jnp.float32)
    grad_chosen = jnp.dot(adjoint_flipped, all_texts, preferred_element_type=jnp.float32)
    grad_images_all = lax.dot_general(
        adjoint_affinity, text_unit, (((0,), (0,)), ((), ())), preferred_element_type=jnp.float32
    )
    grad_images_all = grad_images_all + lax.dot_general(
        positive,
        grad_chosen,
        (((0,), (0,)), ((), ())),
        precision=lax.Precision.HIGHEST,
        preferred_element_type=jnp.float32,
    )
    grad_texts_all = lax.dot_general(
        adjoint_flipped, chosen, (((0,), (0,)), ((), ())), preferred_element_type=jnp.float32
    )
    image_share, text_share = (
        lax.psum_scatter(grad_images_all, ("rep", "fsdp"), scatter_dimension=0, tiled=True),
        lax.psum_scatter(grad_texts_all, ("rep", "fsdp"), scatter_dimension=0, tiled=True),
    )
    sharpness_adjoint = lax.psum(sharpness_contribution, ("rep", "fsdp"))
    _, image_pull = jax.vjp(unit_rows, image_raw)
    grad_image_raw = image_pull(image_share)[0].astype(jnp.bfloat16)
    _, text_pull = jax.vjp(unit_rows, text_raw)
    grad_text_raw = text_pull(text_share + grad_text_here)[0].astype(jnp.bfloat16)
    image_proj_part = outer_sum(pooled_low, grad_image_raw)
    image_bias_part = column_sum(grad_image_raw)
    text_proj_part = outer_sum(caption_low, grad_text_raw)
    text_bias_part = column_sum(grad_text_raw)
    grad_pooled = project_back(grad_image_raw, image_full) / QUERY
    grad_captions = project_back(grad_text_raw, text_full).reshape(captions.shape)
    grad_caption_rows = jnp.sum(picker[:, :, :, None] * grad_captions[:, :, None, :], axis=1)
    grad_query_rows = jnp.broadcast_to(grad_pooled[:, None, :], (row_count, QUERY, model_width))
    grad_final = upstream_adjoint.astype(jnp.float32) + jnp.concatenate(
        [grad_query_rows, grad_caption_rows], axis=1
    )
    feed_again = (
        lax.all_gather(widening_matrix, "fsdp", axis=0, tiled=True),
        lax.all_gather(widening_offset, "fsdp", axis=0, tiled=True),
        lax.all_gather(narrowing_matrix, "fsdp", axis=0, tiled=True),
        lax.all_gather(narrowing_offset, "fsdp", axis=0, tiled=True),
        lax.all_gather(perceptron_center_scale, "fsdp", axis=0, tiled=True),
        lax.all_gather(perceptron_center_shift, "fsdp", axis=0, tiled=True),
    )
    cross_again = (
        lax.all_gather(mixing_asker_matrix, "fsdp", axis=0, tiled=True),
        lax.all_gather(visual_lookup_pairs, "fsdp", axis=0, tiled=True),
        lax.all_gather(mixing_result_matrix, "fsdp", axis=0, tiled=True),
        lax.all_gather(mixing_result_offset, "fsdp", axis=0, tiled=True),
        lax.all_gather(mixing_center_scale, "fsdp", axis=0, tiled=True),
        lax.all_gather(mixing_center_shift, "fsdp", axis=0, tiled=True),
    )
    self_again = (
        lax.all_gather(attend_triple_matrix, "fsdp", axis=0, tiled=True),
        lax.all_gather(inward_result_matrix, "fsdp", axis=0, tiled=True),
        lax.all_gather(inward_result_offset, "fsdp", axis=0, tiled=True),
        lax.all_gather(inward_center_scale, "fsdp", axis=0, tiled=True),
        lax.all_gather(inward_center_shift, "fsdp", axis=0, tiled=True),
    )
    inner_again, self_kept = run_self(self_again, sequence_entries, allowed)
    merged_again, cross_kept = run_cross(cross_again, inner_again, picture_descriptors)
    _, feed_kept = run_feed(feed_again, merged_again)
    grad_merged, feed_partials = feed_back(feed_again, feed_kept, grad_final)
    feed_shares = (
        lax.psum_scatter(feed_partials[0], "fsdp", scatter_dimension=0, tiled=True),
        lax.psum_scatter(feed_partials[1], "fsdp", scatter_dimension=0, tiled=True),
        lax.psum_scatter(feed_partials[2], "fsdp", scatter_dimension=0, tiled=True),
        lax.psum_scatter(feed_partials[3], "fsdp", scatter_dimension=0, tiled=True),
        lax.psum_scatter(feed_partials[4], "fsdp", scatter_dimension=0, tiled=True),
        lax.psum_scatter(feed_partials[5], "fsdp", scatter_dimension=0, tiled=True),
        lax.psum_scatter(image_proj_part, "fsdp", scatter_dimension=0, tiled=True),
        lax.psum_scatter(image_bias_part, "fsdp", scatter_dimension=0, tiled=True),
        lax.psum_scatter(text_proj_part, "fsdp", scatter_dimension=0, tiled=True),
        lax.psum_scatter(text_bias_part, "fsdp", scatter_dimension=0, tiled=True),
    )
    grad_inner, cross_partials = cross_back(
        cross_again, cross_kept, picture_descriptors, grad_merged
    )
    cross_shares = (
        lax.psum_scatter(cross_partials[0], "fsdp", scatter_dimension=0, tiled=True),
        lax.psum_scatter(cross_partials[1], "fsdp", scatter_dimension=0, tiled=True),
        lax.psum_scatter(cross_partials[2], "fsdp", scatter_dimension=0, tiled=True),
        lax.psum_scatter(cross_partials[3], "fsdp", scatter_dimension=0, tiled=True),
        lax.psum_scatter(cross_partials[4], "fsdp", scatter_dimension=0, tiled=True),
        lax.psum_scatter(cross_partials[5], "fsdp", scatter_dimension=0, tiled=True),
    )
    incoming_sequence_adjoint, self_partials = self_back(
        self_again, self_kept, sequence_entries, allowed, grad_inner
    )
    self_shares = (
        lax.psum_scatter(self_partials[0], "fsdp", scatter_dimension=0, tiled=True),
        lax.psum_scatter(self_partials[1], "fsdp", scatter_dimension=0, tiled=True),
        lax.psum_scatter(self_partials[2], "fsdp", scatter_dimension=0, tiled=True),
        lax.psum_scatter(self_partials[3], "fsdp", scatter_dimension=0, tiled=True),
        lax.psum_scatter(self_partials[4], "fsdp", scatter_dimension=0, tiled=True),
    )
    totals = (
        lax.psum(self_shares[0].astype(jnp.bfloat16), "rep").astype(jnp.float32),
        lax.psum(self_shares[1].astype(jnp.bfloat16), "rep").astype(jnp.float32),
        lax.psum(self_shares[2].astype(jnp.bfloat16), "rep").astype(jnp.float32),
        lax.psum(self_shares[3].astype(jnp.bfloat16), "rep").astype(jnp.float32),
        lax.psum(self_shares[4].astype(jnp.bfloat16), "rep").astype(jnp.float32),
        lax.psum(cross_shares[0].astype(jnp.bfloat16), "rep").astype(jnp.float32),
        lax.psum(cross_shares[1].astype(jnp.bfloat16), "rep").astype(jnp.float32),
        lax.psum(cross_shares[2].astype(jnp.bfloat16), "rep").astype(jnp.float32),
        lax.psum(cross_shares[3].astype(jnp.bfloat16), "rep").astype(jnp.float32),
        lax.psum(cross_shares[4].astype(jnp.bfloat16), "rep").astype(jnp.float32),
        lax.psum(cross_shares[5].astype(jnp.bfloat16), "rep").astype(jnp.float32),
        lax.psum(feed_shares[0].astype(jnp.bfloat16), "rep").astype(jnp.float32),
        lax.psum(feed_shares[1].astype(jnp.bfloat16), "rep").astype(jnp.float32),
        lax.psum(feed_shares[2].astype(jnp.bfloat16), "rep").astype(jnp.float32),
        lax.psum(feed_shares[3].astype(jnp.bfloat16), "rep").astype(jnp.float32),
        lax.psum(feed_shares[4].astype(jnp.bfloat16), "rep").astype(jnp.float32),
        lax.psum(feed_shares[5].astype(jnp.bfloat16), "rep").astype(jnp.float32),
        lax.psum(feed_shares[6].astype(jnp.bfloat16), "rep").astype(jnp.float32),
        lax.psum(feed_shares[7].astype(jnp.bfloat16), "rep").astype(jnp.float32),
        lax.psum(feed_shares[8].astype(jnp.bfloat16), "rep").astype(jnp.float32),
        lax.psum(feed_shares[9].astype(jnp.bfloat16), "rep").astype(jnp.float32),
    )
    return (
        finishing_lines.astype(jnp.bfloat16),
        incoming_sequence_adjoint,
        totals[0],
        totals[1],
        totals[2],
        totals[3],
        totals[4],
        totals[5],
        totals[6],
        totals[7],
        totals[8],
        totals[9],
        totals[10],
        totals[11],
        totals[12],
        totals[13],
        totals[14],
        totals[15],
        totals[16],
        totals[17],
        totals[18],
        totals[19],
        totals[20],
        sharpness_adjoint,
    )


def solution(mesh):
    placed = (
        P(("rep", "fsdp"), None, None),
        P(("rep", "fsdp"), None, None),
        P(("rep", "fsdp"), None),
        P(("rep", "fsdp")),
        P(("rep", "fsdp"), None, None),
        P("fsdp", None),
        P("fsdp", None),
        P("fsdp"),
        P("fsdp"),
        P("fsdp"),
        P("fsdp", None),
        P("fsdp", None),
        P("fsdp", None),
        P("fsdp"),
        P("fsdp"),
        P("fsdp"),
        P("fsdp", None),
        P("fsdp"),
        P("fsdp", None),
        P("fsdp"),
        P("fsdp"),
        P("fsdp"),
        P("fsdp", None),
        P("fsdp"),
        P("fsdp", None),
        P("fsdp"),
        P(),
    )
    return jax.shard_map(
        on_device,
        mesh=mesh,
        in_specs=placed,
        out_specs=(
            P(("rep", "fsdp"), None, None),
            P(("rep", "fsdp"), None, None),
            P("fsdp", None),
            P("fsdp", None),
            P("fsdp"),
            P("fsdp"),
            P("fsdp"),
            P("fsdp", None),
            P("fsdp", None),
            P("fsdp", None),
            P("fsdp"),
            P("fsdp"),
            P("fsdp"),
            P("fsdp", None),
            P("fsdp"),
            P("fsdp", None),
            P("fsdp"),
            P("fsdp"),
            P("fsdp"),
            P("fsdp", None),
            P("fsdp"),
            P("fsdp", None),
            P("fsdp"),
            P(),
        ),
        check_vma=False,
    )
```

profile of v0, /device:TPU:0, one launch (start us, length us, event | category | flops | bytes accessed | tf_op | source)
XLA Modules:
  0.0 1839.1 jit_solution(13014052564393894276)
XLA Ops:
  26.7 40.2 %all-reduce.28 = (bf16[768]{0:T(1024)(128)(2,1)S(1)}, bf16[768]{0:T(1024)(128)(2,1)S(1)}, bf16[768]{0:T(1024)(128)(2,1)S(1)}, bf16[768]{0:T(1024)(128)(2,1)S(1)}...) all-reduce(bf16[768]{0:T(1024)(128)(2,1)S(1)} %dynamic-update-slice, ...), channel_id=1, replica_groups=mesh['rep'=4,'fsdp'=8] {'fsdp'}, use_global_device_ids=true, to_apply=%add.1 | all-reduce | flops 7424 | bytes 29696
  67.7 26.4 %all-gather = bf16[8,1,384]{2,1,0:T(2,128)(2,1)S(1)} all-gather(bf16[1,1,384]{2,1,0:T(2,128)(2,1)S(1)} %reshape.354), channel_id=1, replica_groups=mesh['rep'=4,'fsdp'=8] {'fsdp'}, dimensions={0}, use_global_device_ids=true | all-gather | bytes 6912 | tf_op jit(solution)/shard_map/all_gather | solution.py:385
  94.4 33.7 %all_gather.104 = bf16[768,256]{1,0:T(8,128)(2,1)} all-gather(bf16[96,256]{1,0:T(8,128)(2,1)S(1)} %copy-done.74), channel_id=1, replica_groups=mesh['rep'=4,'fsdp'=8] {'fsdp'}, dimensions={0}, use_global_device_ids=true | all-gather | bytes 442368 | tf_op jit(solution)/shard_map/all_gather | solution.py:393
  128.1 33.4 %all_gather.102 = bf16[768,256]{1,0:T(8,128)(2,1)} all-gather(bf16[96,256]{1,0:T(8,128)(2,1)S(1)} %copy-done.75), channel_id=1, replica_groups=mesh['rep'=4,'fsdp'=8] {'fsdp'}, dimensions={0}, use_global_device_ids=true | all-gather | bytes 442368 | tf_op jit(solution)/shard_map/all_gather | solution.py:395
  181.3 59.7 %all-gather.15.cloned.1.call-done = bf16[1408,1536]{1,0:T(8,128)(2,1)} async-done(((bf16[176,1536]{1,0:T(8,128)(2,1)}), bf16[1408,1536]{1,0:T(8,128)(2,1)}) %all-gather.15.cloned.1.call-update) | async-done | bytes 4325392 | tf_op jit(solution)/shard_map/all_gather | solution.py:376
  241.1 9.5 fusion.16
  270.0 12.7 all-gather.19.cloned.1.call-done
  285.9 76.9 %all-gather.21.cloned.1.call-done = bf16[768,3072]{1,0:T(8,128)(2,1)} async-done(((bf16[96,3072]{1,0:T(8,128)(2,1)}), bf16[768,3072]{1,0:T(8,128)(2,1)}) %all-gather.21.cloned.1.call-update) | async-done | bytes 4718608 | tf_op jit(solution)/shard_map/all_gather | solution.py:384
  371.8 14.4 multiply_convert_fusion.1
  386.3 56.4 %all-gather.23.cloned.1.call-done = bf16[3072,768]{1,0:T(8,128)(2,1)} async-done(((bf16[384,768]{1,0:T(8,128)(2,1)}), bf16[3072,768]{1,0:T(8,128)(2,1)}) %all-gather.23.cloned.1.call-update) | async-done | bytes 4718608 | tf_op jit(solution)/shard_map/all_gather | solution.py:386
  454.3 70.8 %all-gather.1 = bf16[32,5,256]{2,1,0:T(8,128)(2,1)} all-gather(bf16[1,5,256]{2,1,0:T(8,128)(2,1)S(1)} %fusion.80), channel_id=1, replica_groups=mesh['rep'=4,'fsdp'=8] {'rep','fsdp'}, dimensions={0}, use_global_device_ids=true | all-gather | bytes 84480 | tf_op jit(solution)/shard_map/all_gather | solution.py:408
  531.5 69.8 %all-gather.2 = bf16[32,10,256]{2,1,0:T(8,128)(2,1)} all-gather(bf16[1,10,256]{2,1,0:T(8,128)(2,1)S(1)} %fusion.175), channel_id=1, replica_groups=mesh['rep'=4,'fsdp'=8] {'rep','fsdp'}, dimensions={0}, use_global_device_ids=true | all-gather | bytes 168960 | tf_op jit(solution)/shard_map/all_gather | solution.py:409
  612.5 125.6 %all-reduce.35.cloned.1.call-done = (f32[320,256]{1,0:T(8,128)}, f32[160,256]{1,0:T(8,128)}) async-done(((f32[320,256]{1,0:T(8,128)}, f32[160,256]{1,0:T(8,128)}), (f32[320,256]{1,0:T(8,128)}, f32[160,256]{1,0:T(8,128)})) %all-reduce.35.cloned.1.call-update) | async-done | bytes 491536
  758.5 9.9 convert_reduce_fusion
  864.0 12.0 convolution_bitcast_fusion
  903.9 38.4 %all-reduce.27 = (bf16[768]{0:T(1024)(128)(2,1)S(1)}, bf16[768]{0:T(1024)(128)(2,1)S(1)}, bf16[768]{0:T(1024)(128)(2,1)S(1)}, bf16[768]{0:T(1024)(128)(2,1)S(1)}...) all-reduce(f32[768]{0:T(1024)S(1)} %get-tuple-element.186, ...), channel_id=6, replica_groups=mesh['rep'=4,'fsdp'=8] {'fsdp'}, use_global_device_ids=true, to_apply=%region_37.38.clone | all-reduce | flops 10496 | bytes 62976
  955.2 70.5 %reduce-scatter.14.cloned.1.call-done = f32[96,768]{1,0:T(8,128)} async-done(((f32[768,768]{1,0:T(8,128)}), f32[96,768]{1,0:T(8,128)}) %reduce-scatter.14.cloned.1.call-update) | async-done | bytes 294928 | tf_op jit(solution)/shard_map/reduce_scatter | solution.py:523
  1027.4 70.7 %reduce-scatter.18.cloned.1.call-done = f32[96,768]{1,0:T(8,128)} async-done(((f32[768,768]{1,0:T(8,128)}), f32[96,768]{1,0:T(8,128)}) %reduce-scatter.18.cloned.1.call-update) | async-done | bytes 294928 | tf_op jit(solution)/shard_map/reduce_scatter | solution.py:513
  1099.8 130.3 %reduce-scatter.28.cloned.1.call-done = f32[96,2304]{1,0:T(8,128)} async-done(((f32[768,2304]{1,0:T(8,128)}), f32[96,2304]{1,0:T(8,128)}) %reduce-scatter.28.cloned.1.call-update) | async-done | bytes 884752
  1232.3 151.6 %reduce-scatter.30.cloned.1.call-done = f32[176,1536]{1,0:T(8,128)} async-done(((f32[1408,1536]{1,0:T(8,128)}), f32[176,1536]{1,0:T(8,128)}) %reduce-scatter.30.cloned.1.call-update) | async-done | bytes 1081360
  1386.3 162.2 %reduce-scatter.22.cloned.1.call-done = f32[384,768]{1,0:T(8,128)} async-done(((f32[3072,768]{1,0:T(8,128)}), f32[384,768]{1,0:T(8,128)}) %reduce-scatter.22.cloned.1.call-update) | async-done | bytes 1179664 | tf_op jit(solution)/shard_map/reduce_scatter | solution.py:498
  1550.7 162.5 %reduce-scatter.20.cloned.1.call-done = f32[96,3072]{1,0:T(8,128)} async-done(((f32[768,3072]{1,0:T(8,128)}), f32[96,3072]{1,0:T(8,128)}) %reduce-scatter.20.cloned.1.call-update) | async-done | bytes 1179664 | tf_op jit(solution)/shard_map/reduce_scatter | solution.py:496
  1719.5 39.6 %psum.175 = f32[]{:T(128)} all-reduce(f32[]{:T(128)S(6)} %add_any.75), channel_id=1, replica_groups=mesh['rep'=4,'fsdp'=8] {'rep','fsdp'}, use_global_device_ids=true, to_apply=%region_91.92 | all-reduce | flops 1 | bytes 8 | tf_op jit(solution)/shard_map/psum | solution.py:452
  1781.7 39.6 %all-reduce.39.cloned.1.call-done = (bf16[96,2304]{0,1:T(8,128)(2,1)}, bf16[176,1536]{0,1:T(8,128)(2,1)}, bf16[96,768]{1,0:T(8,128)(2,1)}, bf16[96,768]{1,0:T(8,...) async-done(((bf16[96,2304]{0,1:T(8,128)(2,1)}, bf16[176,1536]{0,1:T(8,128)(2,1)}, bf16[96,768]{1,0:T(8,128)(2,1)}, ...) | async-done | bytes 2605072 | tf_op jit(solution)/shard_map/psum | solution.py:529
  (474 shorter events, 300.0 us)
Async XLA Ops:
  7.2 154.4 %all-gather.11.cloned.1.call-start = ((), (), s32[]{:S(2)}) async-start(), calls=%async_computation.9 | async-start | bytes 3981312 | tf_op jit(solution)/shard_map/all_gather | solution.py:367
  8.0 165.2 %all-gather.13.cloned.1.call-start = ((), (), s32[]{:S(2)}) async-start(), calls=%async_computation.10 | async-start | bytes 1327104 | tf_op jit(solution)/shard_map/all_gather | solution.py:368
  8.7 169.7 %all-gather.17.cloned.1.call-start = ((), (), s32[]{:S(2)}) async-start(), calls=%async_computation.12 | async-start | bytes 1327104 | tf_op jit(solution)/shard_map/all_gather | solution.py:375
  9.4 231.6 %all-gather.15.cloned.1.call-start = ((), (), s32[]{:S(2)}) async-start(), calls=%async_computation.11 | async-start | bytes 4866048 | tf_op jit(solution)/shard_map/all_gather | solution.py:376
  10.0 272.7 %all-gather.19.cloned.1.call-start = ((), (), s32[]{:S(2)}) async-start(), calls=%async_computation.13 | async-start | bytes 1327104 | tf_op jit(solution)/shard_map/all_gather | solution.py:377
  10.6 352.2 %all-gather.21.cloned.1.call-start = ((), (), s32[]{:S(2)}) async-start(), calls=%async_computation.14 | async-start | bytes 5308416 | tf_op jit(solution)/shard_map/all_gather | solution.py:384
  11.2 431.5 %all-gather.23.cloned.1.call-start = ((), (), s32[]{:S(2)}) async-start(), calls=%async_computation.15 | async-start | bytes 5308416 | tf_op jit(solution)/shard_map/all_gather | solution.py:386
  11.9 726.1 %all-reduce.35.cloned.1.call-start = ((), (), s32[]{:S(2)}) async-start(), calls=%async_computation.25 | async-start | bytes 983040
  67.6 381.6 %copy-start.68 = (f32[768]{0:T(1024)}, f32[768]{0:T(1024)S(1)}, u32[]{:S(2)}) copy-start(f32[768]{0:T(1024)S(1)} %convert_element_type.367) | copy-start | bytes 9220
  67.7 383.6 %copy-start.76 = (f32[5,2,64]{2,1,0:T(2,128)}, f32[5,2,64]{2,1,0:T(2,128)S(1)}, u32[]{:S(2)}) copy-start(f32[5,2,64]{2,1,0:T(2,128)S(1)} %compare_convert_fusion) | copy-start | bytes 7684
  611.6 337.9 %reduce-scatter.24.cloned.1.call-start = ((), (), s32[]{:S(2)}) async-start(), calls=%async_computation.21 | async-start | bytes 884736 | tf_op jit(solution)/shard_map/reduce_scatter | solution.py:502
  752.0 199.1 %reduce-scatter.26.cloned.1.call-start = ((), (), s32[]{:S(2)}) async-start(), calls=%async_computation.22 | async-start | bytes 884736 | tf_op jit(solution)/shard_map/reduce_scatter | solution.py:504
  774.4 179.2 %reduce-scatter.16.cloned.1.call-start = ((), (), s32[]{:S(2)}) async-start(), calls=%async_computation.17 | async-start | bytes 2654208 | tf_op jit(solution)/shard_map/reduce_scatter | solution.py:511
  792.4 233.4 %reduce-scatter.14.cloned.1.call-start = ((), (), s32[]{:S(2)}) async-start(), calls=%async_computation.16 | async-start | bytes 2654208 | tf_op jit(solution)/shard_map/reduce_scatter | solution.py:523
  803.2 294.9 %reduce-scatter.18.cloned.1.call-start = ((), (), s32[]{:S(2)}) async-start(), calls=%async_computation.18 | async-start | bytes 2654208 | tf_op jit(solution)/shard_map/reduce_scatter | solution.py:513
  805.2 424.9 %reduce-scatter.28.cloned.1.call-start = ((), (), s32[]{:S(2)}) async-start(), calls=%async_computation.23 | async-start | bytes 7962624
  848.1 535.8 %reduce-scatter.30.cloned.1.call-start = ((), (), s32[]{:S(2)}) async-start(), calls=%async_computation.24 | async-start | bytes 9732096
  885.4 663.1 %reduce-scatter.22.cloned.1.call-start = ((), (), s32[]{:S(2)}) async-start(), calls=%async_computation.20 | async-start | bytes 10616832 | tf_op jit(solution)/shard_map/reduce_scatter | solution.py:498
  893.4 819.8 %reduce-scatter.20.cloned.1.call-start = ((), (), s32[]{:S(2)}) async-start(), calls=%async_computation.19 | async-start | bytes 10616832 | tf_op jit(solution)/shard_map/reduce_scatter | solution.py:496
  901.8 863.0 %all-reduce.37.cloned.1.call-start = ((), (), s32[]{:S(2)}) async-start(), calls=%async_computation.26 | async-start | bytes 209920 | tf_op jit(solution)/shard_map/psum | solution.py:531
  952.6 868.8 %all-reduce.39.cloned.1.call-start = ((), (), s32[]{:S(2)}) async-start(), calls=%async_computation.27 | async-start | bytes 5996544 | tf_op jit(solution)/shard_map/psum | solution.py:529
  1386.3 372.8 %copy-start.16 = (f32[5,96,768]{2,1,0:T(8,128)S(1)}, f32[5,96,768]{2,1,0:T(8,128)}, u32[]{:S(2)}) copy-start(f32[5,96,768]{2,1,0:T(8,128)} %copy-done.15) | copy-start | bytes 4423684
  1386.3 372.8 %copy-start.38 = (bf16[5,96,768]{2,1,0:T(8,128)(2,1)S(1)}, bf16[5,96,768]{2,1,0:T(8,128)(2,1)}, u32[]{:S(2)}) copy-start(bf16[5,96,768]{2,1,0:T(8,128)(2,1)} %copy.147) | copy-start | bytes 2211844
  1386.3 372.8 %copy-start.39 = (bf16[5,96,768]{2,1,0:T(8,128)(2,1)S(1)}, bf16[5,96,768]{2,1,0:T(8,128)(2,1)}, u32[]{:S(2)}) copy-start(bf16[5,96,768]{2,1,0:T(8,128)(2,1)} %copy.145) | copy-start | bytes 2211844
  (104 other events, 3997.4 us)
Sparse Core Ops, SparseCore 0:
  10.2 68.0 all-gather.10
  80.5 41.7 all-gather.12
  124.5 40.8 all-gather.16
  167.5 73.5 all-gather.14
  243.1 39.6 all-gather.18
  284.8 78.0 all-gather.20
  365.0 77.6 all-gather.22
  611.7 126.2 all-reduce.34
  752.1 63.4 reduce-scatter.23
  818.7 62.2 reduce-scatter.25
  884.5 69.0 reduce-scatter.15
  957.0 68.7 reduce-scatter.13
  1029.3 68.8 reduce-scatter.17
  1101.7 128.3 reduce-scatter.27
  1233.5 150.2 reduce-scatter.29
  1387.3 161.1 reduce-scatter.21
  1552.0 161.1 reduce-scatter.19
  1718.2 31.2 all-reduce.36
  1753.6 67.6 all-reduce.38
where the time goes:
time: 1850 us; the launch traced here: 1840 us
  waiting for transfers between devices  1120 us (61%)
  blocking collectives  352 us (19%)
  matrix products  147 us (8%)
  local copies, waits for them, and re-layouts  106 us (6%)
  other arithmetic  86.2 us (5%)
  between operations  22 us (1%)
    unnamed x22, waiting for transfers between devices  412 us
    reduce_scatter x1, waiting for transfers between devices, on_device(): lax.psum_scatter(feed_partials[0], 'fsdp', scatter_dimension=0, tiled=True)  163 us
    reduce_scatter x1, waiting for transfers between devices, on_device(): lax.psum_scatter(feed_partials[2], 'fsdp', scatter_dimension=0, tiled=True)  162 us
    unnamed x2, blocking collectives  78.6 us
    all_gather x1, waiting for transfers between devices, on_device(): lax.all_gather(widening_matrix, 'fsdp', axis=0, tiled=True)  76.9 us
    all_gather x1, blocking collectives, on_device(): lax.all_gather(image_unit, ('rep', 'fsdp'), axis=0, tiled=True)  70.8 us
    reduce_scatter x1, waiting for transfers between devices, on_device(): lax.psum_scatter(cross_partials[2], 'fsdp', scatter_dimension=0, tiled=True)  70.7 us
    reduce_scatter x1, waiting for transfers between devices, on_device(): lax.psum_scatter(self_partials[1], 'fsdp', scatter_dimension=0, tiled=True)  70.5 us
  transfers between devices with their start and end apart: 19, of which 13 were waited for; matrix products, arithmetic and copies ran while one was open for 15% of the time, Pallas kernels for 0%

commit v1 on v0

v1 whole, which is shorter than its diff:
```python
from functools import partial

import jax
import jax.numpy as jnp
from jax import lax
from jax.sharding import PartitionSpec as P

HEADS = 12
HEAD = 64
QUERY = 32
CAPS_ROW = 2


def project(values, matrix):
    return jnp.einsum("...d,df->...f", values, matrix, preferred_element_type=jnp.float32)


def project_back(gradient, matrix):
    return jnp.einsum("...f,df->...d", gradient, matrix, preferred_element_type=jnp.float32)


def outer_sum(values, gradient):
    flat_values = values.reshape(-1, values.shape[-1])
    flat_gradient = gradient.reshape(-1, gradient.shape[-1])
    return lax.dot_general(
        flat_values, flat_gradient, (((0,), (0,)), ((), ())), preferred_element_type=jnp.float32
    )


def column_sum(gradient):
    return jnp.sum(gradient.reshape(-1, gradient.shape[-1]), axis=0, dtype=jnp.float32)


def layer_norm(summed, norm_gain, norm_shift):
    center = summed - jnp.mean(summed, axis=-1, keepdims=True)
    spread = jnp.mean(center * center, axis=-1, keepdims=True)
    return center * lax.rsqrt(spread + 1e-06) * norm_gain + norm_shift


def norm_back(summed, norm_gain, norm_shift, gradient):
    _, reverse_sweep_rule = jax.vjp(layer_norm, summed, norm_gain, norm_shift)
    return reverse_sweep_rule(gradient)


def unit_rows(values):
    return values * lax.rsqrt(jnp.sum(values * values, axis=-1, keepdims=True) + 1e-06)


def exact_gelu(values):
    return jax.nn.gelu(values, approximate=False)


def token_kinds(sentence_numbering):
    query_kinds = jnp.zeros((sentence_numbering.shape[0], QUERY), jnp.int32)
    return jnp.concatenate([query_kinds, sentence_numbering + 1], axis=1)


def caption_picker(sentence_numbering):
    caption_ids = jnp.arange(CAPS_ROW, dtype=jnp.int32)
    starts = jnp.sum(
        (sentence_numbering[:, None, :] < caption_ids[None, :, None]).astype(jnp.int32), axis=2
    )
    places = jnp.arange(sentence_numbering.shape[1], dtype=jnp.int32)
    return (places[None, None, :] == starts[:, :, None]).astype(jnp.float32)


def split_heads(values):
    return values.reshape(values.shape[0], values.shape[1], HEADS, values.shape[2] // HEADS)


def scores_of(queries, key_rows, allowed):
    scaling = HEAD ** (-0.5)
    scores = (
        jnp.einsum(
            "bqhd,bkhd->bhqk",
            split_heads(queries),
            split_heads(key_rows),
            preferred_element_type=jnp.float32,
        )
        * scaling
    )
    if allowed is not None:
        scores = jnp.where(allowed[:, None], scores, -1e30)
    return (scores, scaling)


def swap(values, axis, step):
    count = lax.axis_size(axis)
    return lax.ppermute(values, axis, [(i, i ^ step) for i in range(count)])


def bit_of(axis, step):
    return (lax.axis_index(axis) // step) % 2


def bits(axis):
    count = lax.axis_size(axis)
    assert count & (count - 1) == 0
    return [1 << k for k in range(count.bit_length() - 1)]


def route(first):
    rep = [("rep", step) for step in bits("rep")[1:]]
    fsdp = [("fsdp", step) for step in bits("fsdp")]
    return rep + fsdp if first == "rep" else fsdp[:1] + rep + fsdp[1:]


def shard_sum(values, gradient, first):
    flat_values = values.reshape(-1, values.shape[-1])
    flat_gradient = gradient.reshape(-1, gradient.shape[-1])
    half = flat_gradient.shape[1] // 2
    core = bit_of("rep", 1)
    other = lax.dynamic_slice_in_dim(flat_gradient, (1 - core) * half, half, 1)
    mine = lax.dynamic_slice_in_dim(flat_gradient, core * half, half, 1)
    sent = outer_sum(flat_values, other).astype(jnp.bfloat16)
    kept = outer_sum(flat_values, mine).astype(jnp.bfloat16)
    return halves(sent, kept, first)


def halves(sent, kept, first):
    total = add(kept, swap(sent, "rep", 1))
    fsdp = [("fsdp", step) for step in reversed(bits("fsdp"))]
    rep = [("rep", step) for step in reversed(bits("rep")[1:])]
    places = fsdp + rep
    rows = total.shape[0] // 2 ** len(places)
    total = total.reshape((2,) * len(places) + (rows, total.shape[1]))
    for axis, step in route(first):
        at = places.index((axis, step))
        here = bit_of(axis, step)
        away = lax.dynamic_index_in_dim(total, 1 - here, at, False)
        stay = lax.dynamic_index_in_dim(total, here, at, False)
        total = add(stay, swap(away, axis, step))
        places = places[:at] + places[at + 1 :]
    return total


def add(left, right):
    return (left.astype(jnp.float32) + right.astype(jnp.float32)).astype(jnp.bfloat16)


def whole_shard(piece):
    every = lax.all_gather(piece, "rep", axis=0, tiled=False)
    rows, columns = piece.shape
    every = every.reshape(-1, 2, rows, columns).transpose(0, 2, 1, 3)
    return every.reshape(-1, 2 * columns).astype(jnp.float32)


def gather_rows(shard):
    part = shard.shape[0] // lax.axis_size("rep")
    mine = lax.dynamic_slice_in_dim(shard, lax.axis_index("rep") * part, part, 0)
    return lax.all_gather(mine, ("fsdp", "rep"), axis=0, tiled=True)


def gather_columns(shard):
    count = lax.axis_size("rep")
    part = shard.shape[1] // count
    mine = lax.dynamic_slice_in_dim(shard, lax.axis_index("rep") * part, part, 1)
    whole = lax.all_gather(mine, ("rep", "fsdp"), axis=0, tiled=True)
    return whole.reshape(count, -1, part)


def attend(queries, key_rows, value_rows, allowed):
    scores, _ = scores_of(queries, key_rows, allowed)
    highest = jnp.max(scores, axis=-1, keepdims=True)
    exponent = jnp.exp(scores - highest)
    normalizer = jnp.sum(exponent, axis=-1, keepdims=True)
    probs = exponent / normalizer
    mixed_heads = jnp.einsum(
        "bhqk,bkhd->bqhd",
        probs.astype(jnp.bfloat16),
        split_heads(value_rows),
        preferred_element_type=jnp.float32,
    )
    mixed_heads = mixed_heads.reshape(queries.shape[0], queries.shape[1], -1).astype(jnp.bfloat16)
    return (mixed_heads, probs)


def attend_back(queries, key_rows, value_rows, attention_probs, grad_mixed):
    scaling = HEAD ** (-0.5)
    upstream = split_heads(grad_mixed)
    grad_value = jnp.einsum(
        "bhqk,bqhd->bkhd",
        attention_probs.astype(jnp.bfloat16),
        upstream,
        preferred_element_type=jnp.float32,
    )
    grad_probs = jnp.einsum(
        "bqhd,bkhd->bhqk", upstream, split_heads(value_rows), preferred_element_type=jnp.float32
    )
    grad_scores = attention_probs * (
        grad_probs - jnp.sum(attention_probs * grad_probs, axis=-1, keepdims=True)
    )
    grad_scores = grad_scores.astype(jnp.bfloat16)
    grad_query = (
        jnp.einsum(
            "bhqk,bkhd->bqhd",
            grad_scores,
            split_heads(key_rows),
            preferred_element_type=jnp.float32,
        )
        * scaling
    )
    grad_key = (
        jnp.einsum(
            "bhqk,bqhd->bkhd", grad_scores, split_heads(queries), preferred_element_type=jnp.float32
        )
        * scaling
    )
    batch = queries.shape[0]
    return (
        grad_query.reshape(batch, queries.shape[1], -1),
        grad_key.reshape(batch, key_rows.shape[1], -1),
        grad_value.reshape(batch, key_rows.shape[1], -1),
    )


def contrast(similar, reverse_sims, temper, positive, caption_total):
    image_side = jax.nn.logsumexp(similar / temper, axis=-1)
    text_side = jax.nn.logsumexp(reverse_sims / temper, axis=-1)
    matched = jnp.sum(similar * positive, axis=-1) / temper
    return jnp.sum(image_side + text_side - 2.0 * matched) / (2.0 * caption_total)


def on_device(
    sequence_entries,
    picture_descriptors,
    sentence_numbering,
    sentence_picture_owner,
    upstream_adjoint,
    attend_triple_matrix,
    inward_result_matrix,
    inward_result_offset,
    inward_center_scale,
    inward_center_shift,
    mixing_asker_matrix,
    visual_lookup_pairs,
    mixing_result_matrix,
    mixing_result_offset,
    mixing_center_scale,
    mixing_center_shift,
    widening_matrix,
    widening_offset,
    narrowing_matrix,
    narrowing_offset,
    perceptron_center_scale,
    perceptron_center_shift,
    picture_mapping_matrix,
    picture_vector_offset,
    sentence_mapping_matrix,
    sentence_vector_offset,
    logit_sharpness,
):
    f32 = jnp.float32
    bf16 = jnp.bfloat16
    everywhere = ("rep", "fsdp")
    rows, row_len, width = sequence_entries.shape
    segment_of = token_kinds(sentence_numbering)
    allowed = segment_of[:, :, None] == segment_of[:, None, :]
    picker = caption_picker(sentence_numbering)

    vectors = (
        inward_result_offset,
        inward_center_scale,
        inward_center_shift,
        mixing_result_offset,
        mixing_center_scale,
        mixing_center_shift,
        widening_offset,
        narrowing_offset,
        perceptron_center_scale,
        perceptron_center_shift,
        picture_vector_offset,
        sentence_vector_offset,
    )
    packed = lax.all_gather(jnp.concatenate(vectors), "fsdp", axis=0, tiled=False)
    spread = []
    offset = 0
    for vector in vectors:
        size = vector.shape[0]
        spread.append(packed[:, offset : offset + size].reshape(-1).astype(f32))
        offset += size
    (
        self_offset,
        self_scale,
        self_shift,
        cross_offset,
        cross_scale,
        cross_shift,
        wide_offset,
        narrow_offset,
        feed_scale,
        feed_shift,
        image_shift,
        text_shift,
    ) = spread
    owners = lax.all_gather(sentence_picture_owner, everywhere, axis=0, tiled=True)

    w_qkv = gather_rows(attend_triple_matrix)
    w_self_out = gather_rows(inward_result_matrix)
    w_keyval = gather_columns(visual_lookup_pairs)
    w_asker = gather_rows(mixing_asker_matrix)
    w_cross_out = gather_rows(mixing_result_matrix)
    w_up = gather_rows(widening_matrix)
    w_down = gather_rows(narrowing_matrix)
    w_ends = gather_rows(jnp.concatenate([picture_mapping_matrix, sentence_mapping_matrix], axis=1))
    emb = picture_mapping_matrix.shape[1]
    w_image = w_ends[:, :emb]
    w_text = w_ends[:, emb:]

    qkv = project(sequence_entries, w_qkv).astype(bf16)
    q_self, k_self, v_self = (qkv[..., i * width : (i + 1) * width] for i in range(3))
    self_mix, self_probs = attend(q_self, k_self, v_self, allowed)
    first_sum = sequence_entries.astype(f32) + project(self_mix, w_self_out) + self_offset
    inner = layer_norm(first_sum, self_scale, self_shift)

    head_rows = inner[:, :QUERY]
    head_low = head_rows.astype(bf16)
    asked = project(head_low, w_asker).astype(bf16)
    parts = w_keyval.shape[0]
    keyval = jnp.concatenate(
        [project(picture_descriptors, w_keyval[i]).astype(bf16) for i in range(parts)], axis=-1
    )
    k_cross, v_cross = keyval[..., :width], keyval[..., width:]
    cross_mix, cross_probs = attend(asked, k_cross, v_cross, None)
    second_sum = head_rows + project(cross_mix, w_cross_out) + cross_offset
    normed = layer_norm(second_sum, cross_scale, cross_shift)
    merged = jnp.concatenate([normed, inner[:, QUERY:]], axis=1)

    merged_low = merged.astype(bf16)
    pre_act = project(merged_low, w_up) + wide_offset
    activated = exact_gelu(pre_act).astype(bf16)
    third_sum = merged + project(activated, w_down) + narrow_offset
    final = layer_norm(third_sum, feed_scale, feed_shift)
    out = final.astype(bf16)

    pooled_low = jnp.mean(final[:, :QUERY], axis=1).astype(bf16)
    image_raw = project(pooled_low, w_image) + image_shift
    image_unit = unit_rows(image_raw).astype(bf16)
    caption_low = jnp.einsum(
        "rcp,rpd->rcd", picker.astype(bf16), out[:, QUERY:], preferred_element_type=f32
    )
    caption_low = caption_low.astype(bf16).reshape(-1, width)
    text_raw = project(caption_low, w_text) + text_shift
    text_unit = unit_rows(text_raw).astype(bf16)
    units = lax.all_gather(
        jnp.concatenate([image_unit, text_unit], axis=0), everywhere, axis=0, tiled=False
    )
    all_images = units[:, :rows].reshape(-1, emb)
    all_texts = units[:, rows:].reshape(-1, emb)
    image_total = all_images.shape[0]
    text_total = all_texts.shape[0]
    positive = owners[:, None] == jnp.arange(image_total, dtype=jnp.int32)[None, :]
    similar = lax.dot_general(
        all_texts, all_images, (((1,), (1,)), ((), ())), preferred_element_type=f32
    )
    chosen = jnp.dot(positive.astype(bf16), all_images, preferred_element_type=f32).astype(bf16)
    reverse_sims = lax.dot_general(
        chosen, all_texts, (((1,), (1,)), ((), ())), preferred_element_type=f32
    )
    _, contrast_pull = jax.vjp(
        partial(contrast, positive=positive.astype(f32), caption_total=text_total),
        similar,
        reverse_sims,
        logit_sharpness,
    )
    grad_sims, grad_back, sharpness_adjoint = contrast_pull(jnp.ones((), f32))
    grad_sims = grad_sims.astype(bf16)
    grad_back = grad_back.astype(bf16)
    device = lax.axis_index("rep") * lax.axis_size("fsdp") + lax.axis_index("fsdp")
    texts_here = text_unit.shape[0]
    grad_chosen = jnp.dot(grad_back, all_texts, preferred_element_type=f32)
    own_images = device * rows + jnp.arange(rows, dtype=jnp.int32)
    own_positive = (owners[:, None] == own_images[None, :]).astype(f32)
    own_columns = lax.dynamic_slice_in_dim(grad_sims, device * rows, rows, 1)
    grad_image_unit = outer_sum(own_columns, all_texts) + lax.dot_general(
        own_positive,
        grad_chosen,
        (((0,), (0,)), ((), ())),
        precision=lax.Precision.HIGHEST,
        preferred_element_type=f32,
    )
    own_rows = lax.dynamic_slice_in_dim(grad_sims, device * texts_here, texts_here, 0)
    own_back = lax.dynamic_slice_in_dim(grad_back, device * texts_here, texts_here, 1)
    grad_text_unit = jnp.dot(own_rows, all_images, preferred_element_type=f32) + outer_sum(
        own_back, chosen
    )
    _, image_pull = jax.vjp(unit_rows, image_raw)
    grad_image_raw = image_pull(grad_image_unit)[0].astype(bf16)
    _, text_pull = jax.vjp(unit_rows, text_raw)
    grad_text_raw = text_pull(grad_text_unit)[0].astype(bf16)
    grad_pooled = project_back(grad_image_raw, w_image) / QUERY
    grad_captions = project_back(grad_text_raw, w_text).reshape(rows, CAPS_ROW, width)
    grad_caption_rows = jnp.sum(picker[:, :, :, None] * grad_captions[:, :, None, :], axis=1)
    grad_query_rows = jnp.broadcast_to(grad_pooled[:, None, :], (rows, QUERY, width))
    grad_final = upstream_adjoint.astype(f32) + jnp.concatenate(
        [grad_query_rows, grad_caption_rows], axis=1
    )

    grad_third_sum, feed_gain, feed_shift_grad = norm_back(
        third_sum, feed_scale, feed_shift, grad_final
    )
    grad_third = grad_third_sum.astype(bf16)
    down_piece = shard_sum(activated, grad_third, "fsdp")
    grad_active = project_back(grad_third, w_down)
    _, gelu_pull = jax.vjp(exact_gelu, pre_act)
    grad_pre = gelu_pull(grad_active)[0].astype(bf16)
    up_piece = shard_sum(merged_low, grad_pre, "rep")
    grad_merged = grad_third_sum + project_back(grad_pre, w_up)
    ends = jnp.concatenate(
        [outer_sum(pooled_low, grad_image_raw), outer_sum(caption_low, grad_text_raw)], axis=1
    ).astype(bf16)
    core = bit_of("rep", 1)
    ends_sent = lax.dynamic_slice_in_dim(ends, (1 - core) * emb, emb, 1)
    ends_kept = lax.dynamic_slice_in_dim(ends, core * emb, emb, 1)
    ends_piece = halves(ends_sent, ends_kept, "fsdp")

    grad_second_sum, cross_gain, cross_shift_grad = norm_back(
        second_sum, cross_scale, cross_shift, grad_merged[:, :QUERY]
    )
    grad_second = grad_second_sum.astype(bf16)
    grad_cross_mix = project_back(grad_second, w_cross_out).astype(bf16)
    cross_out_piece = shard_sum(cross_mix, grad_second, "fsdp")
    grad_asked, grad_key, grad_value = attend_back(
        asked, k_cross, v_cross, cross_probs, grad_cross_mix
    )
    grad_asked = grad_asked.astype(bf16)
    grad_keyval = jnp.concatenate([grad_key, grad_value], axis=-1).astype(bf16)
    keyval_piece = shard_sum(picture_descriptors, grad_keyval, "rep")
    asker_piece = shard_sum(head_low, grad_asked, "fsdp")
    grad_head = grad_second_sum + project_back(grad_asked, w_asker)
    grad_inner = jnp.concatenate([grad_head, grad_merged[:, QUERY:]], axis=1)

    grad_first_sum, self_gain, self_shift_grad = norm_back(
        first_sum, self_scale, self_shift, grad_inner
    )
    grad_first = grad_first_sum.astype(bf16)
    self_out_piece = shard_sum(self_mix, grad_first, "rep")
    grad_self_mix = project_back(grad_first, w_self_out).astype(bf16)
    grad_q, grad_k, grad_v = attend_back(q_self, k_self, v_self, self_probs, grad_self_mix)
    grad_qkv = jnp.concatenate([grad_q, grad_k, grad_v], axis=-1).astype(bf16)
    qkv_piece = shard_sum(sequence_entries, grad_qkv, "fsdp")
    incoming = grad_first_sum + project_back(grad_qkv, w_qkv)

    early = (
        column_sum(grad_pre),
        column_sum(grad_third),
        feed_gain,
        feed_shift_grad,
        column_sum(grad_second),
        cross_gain,
        cross_shift_grad,
        column_sum(grad_image_raw),
        column_sum(grad_text_raw),
    )
    late = (column_sum(grad_first), self_gain, self_shift_grad)
    shards = []
    for group in (early, late):
        summed = lax.psum(jnp.concatenate(group), everywhere)
        offset = 0
        for vector in group:
            size = vector.shape[0]
            share = size // lax.axis_size("fsdp")
            start = offset + lax.axis_index("fsdp") * share
            shards.append(lax.dynamic_slice_in_dim(summed, start, share, 0))
            offset += size
    (
        up_bias,
        down_bias,
        feed_gain,
        feed_shift_grad,
        cross_bias,
        cross_gain,
        cross_shift_grad,
        image_bias,
        text_bias,
        self_bias,
        self_gain,
        self_shift_grad,
    ) = shards
    ends_shard = whole_shard(ends_piece)
    return (
        out,
        incoming,
        whole_shard(qkv_piece),
        whole_shard(self_out_piece),
        self_bias,
        self_gain,
        self_shift_grad,
        whole_shard(asker_piece),
        whole_shard(keyval_piece),
        whole_shard(cross_out_piece),
        cross_bias,
        cross_gain,
        cross_shift_grad,
        whole_shard(up_piece),
        up_bias,
        whole_shard(down_piece),
        down_bias,
        feed_gain,
        feed_shift_grad,
        ends_shard[:, :emb],
        image_bias,
        ends_shard[:, emb:],
        text_bias,
        sharpness_adjoint,
    )


def solution(mesh):
    placed = (
        P(("rep", "fsdp"), None, None),
        P(("rep", "fsdp"), None, None),
        P(("rep", "fsdp"), None),
        P(("rep", "fsdp")),
        P(("rep", "fsdp"), None, None),
        P("fsdp", None),
        P("fsdp", None),
        P("fsdp"),
        P("fsdp"),
        P("fsdp"),
        P("fsdp", None),
        P("fsdp", None),
        P("fsdp", None),
        P("fsdp"),
        P("fsdp"),
        P("fsdp"),
        P("fsdp", None),
        P("fsdp"),
        P("fsdp", None),
        P("fsdp"),
        P("fsdp"),
        P("fsdp"),
        P("fsdp", None),
        P("fsdp"),
        P("fsdp", None),
        P("fsdp"),
        P(),
    )
    return jax.shard_map(
        on_device,
        mesh=mesh,
        in_specs=placed,
        out_specs=(
            P(("rep", "fsdp"), None, None),
            P(("rep", "fsdp"), None, None),
            P("fsdp", None),
            P("fsdp", None),
            P("fsdp"),
            P("fsdp"),
            P("fsdp"),
            P("fsdp", None),
            P("fsdp", None),
            P("fsdp", None),
            P("fsdp"),
            P("fsdp"),
            P("fsdp"),
            P("fsdp", None),
            P("fsdp"),
            P("fsdp", None),
            P("fsdp"),
            P("fsdp"),
            P("fsdp"),
            P("fsdp", None),
            P("fsdp"),
            P("fsdp", None),
            P("fsdp"),
            P(),
        ),
        check_vma=False,
    )
```

time: 1850 us -> 992 us (0.54)
  waiting for transfers between devices: 1120 us -> 298 us
  blocking collectives: 352 us -> 275 us
  starting transfers between devices: 1.23 us -> 48.3 us
  local copies, waits for them, and re-layouts: 106 us -> 141 us
  other arithmetic: 86.2 us -> 58.2 us
    reduce_scatter x7 -> x0, waiting for transfers between devices: 467 us -> none  [the longest x1 163 us: on_device(): lax.psum_scatter(feed_partials[0], 'fsdp', scatter_dimension=0, tiled=True)]
    unnamed x22 -> x7, waiting for transfers between devices: 412 us -> 0.11 us
    ppermute x0 -> x40, waiting for transfers between devices: none -> 122 us  [swap(): return lax.ppermute(values, axis, [(i, i ^ step) for i in range(count)])]
    all_gather x5 -> x10, blocking collectives: 234 us -> 161 us  [the longest x1 67.6 us: on_device(): lax.all_gather(jnp.concatenate([image_unit, text_unit], axis=0), everywhe...]
    ppermute x0 -> x40, starting transfers between devices: none -> 48 us  [swap(): return lax.ppermute(values, axis, [(i, i ^ step) for i in range(count)])]
    psum x2 -> x0, waiting for transfers between devices: 39.6 us -> none  [the longest x1 39.6 us: on_device(): lax.psum(self_shares[0].astype(jnp.bfloat16), 'rep').astype(jnp.float32)]
    concatenate x0 -> x11, local copies, waits for them, and re-layouts: none -> 38.5 us  [the longest x3 13.3 us: on_device(): grad_keyval = jnp.concatenate([grad_key, grad_value], axis=-1).astype(bf16)]
    unnamed x262 -> x288, local copies, waits for them, and re-layouts: 62.2 us -> 26.1 us
  transfers between devices with their start and end apart: 19 -> 47, of which waited for: 13 -> 26; matrix products, arithmetic and copies ran while one was open for 15% -> 22% of each run, Pallas kernels for 0% -> 0%
where the time goes in v1:
time: 992 us; the launch traced here: 987 us
  waiting for transfers between devices  298 us (30%)
  blocking collectives  275 us (28%)
  matrix products  145 us (15%)
  local copies, waits for them, and re-layouts  141 us (14%)
  other arithmetic  58.2 us (6%)
  starting transfers between devices  48.3 us (5%)
  between operations  21.4 us (2%)
    ppermute x40, waiting for transfers between devices, swap(): return lax.ppermute(values, axis, [(i, i ^ step) for i in range(count)])  122 us
    all_gather x6, waiting for transfers between devices, gather_rows(): return lax.all_gather(mine, ('fsdp', 'rep'), axis=0, tiled=True)  121 us
    unnamed x2, blocking collectives  76.5 us
    all_gather x1, blocking collectives, on_device(): lax.all_gather(jnp.concatenate([image_unit, text_unit], axis=0), everywhe...  67.6 us
    all_gather x1, waiting for transfers between devices, gather_columns(): whole = lax.all_gather(mine, ('rep', 'fsdp'), axis=0, tiled=True)  54.8 us
    all_gather x8, blocking collectives, whole_shard(): every = lax.all_gather(piece, 'rep', axis=0, tiled=False)  50.7 us
    ppermute x40, starting transfers between devices, swap(): return lax.ppermute(values, axis, [(i, i ^ step) for i in range(count)])  48 us
    dot_general x18, matrix products, outer_sum(): lax.dot_general(flat_values, flat_gradient, (((0,), (0,)), ((), ())), pre...  45.6 us
  transfers between devices with their start and end apart: 47, of which 26 were waited for; matrix products, arithmetic and copies ran while one was open for 22% of the time, Pallas kernels for 0%

profile of v1, /device:TPU:0, one launch (start us, length us, event | category | flops | bytes accessed | tf_op | source)
XLA Modules:
  0.0 987.0 jit_solution(8308928640445047008)
XLA Ops:
  19.3 8.1 concatenate.62
  27.7 39.1 %all-reduce.1 = bf16[10496]{0:T(1024)(128)(2,1)S(1)} all-reduce(bf16[10496]{0:T(1024)(128)(2,1)S(1)} %dynamic-update-slice), channel_id=2, replica_groups=mesh['rep'=4,'fsdp'=8] {'fsdp'}, use_global_device_ids=true, to_apply=%add.1 | all-reduce | flops 10496 | bytes 41984
  72.6 42.8 %all_gather.97 = bf16[768,512]{1,0:T(8,128)(2,1)} all-gather(bf16[24,512]{1,0:T(8,128)(2,1)S(1)} %fusion.151), channel_id=1, replica_groups=mesh['rep'=4,'fsdp'=8] {'fsdp','rep'}, dimensions={0}, use_global_device_ids=true | all-gather | bytes 811008 | tf_op jit(solution)/shard_map/all_gather | solution.py:151
  117.0 37.4 %all-reduce.2 = s32[320]{0:T(512)} all-reduce(s32[320]{0:T(512)S(1)} %dynamic-update-slice.1), channel_id=1, replica_groups=mesh['rep'=4,'fsdp'=8] {'rep','fsdp'}, use_global_device_ids=true, to_apply=%add.2 | all-reduce | flops 320 | bytes 2560
  177.8 10.1 %all-gather.25.cloned.1.call-done = bf16[768,768]{1,0:T(8,128)(2,1)} async-done(((bf16[24,768]{1,0:T(8,128)(2,1)}), bf16[768,768]{1,0:T(8,128)(2,1)}) %all-gather.25.cloned.1.call-update) | async-done | bytes 1179664 | tf_op jit(solution)/shard_map/all_gather | solution.py:151
  197.4 54.8 %all-gather.23.cloned.1.call-done = bf16[5632,384]{1,0:T(8,128)(2,1)} async-done(((bf16[176,384]{1,0:T(8,128)(2,1)}), bf16[5632,384]{1,0:T(8,128)(2,1)}) %all-gather.23.cloned.1.call-update) | async-done | bytes 4325392 | tf_op jit(solution)/shard_map/all_gather | solution.py:158
  283.3 10.8 %fusion.196 = (f32[5,12,32]{2,1,0:T(8,128)S(1)}, f32[5,12,32,257]{3,2,1,0:T(8,128)S(1)}) fusion(f32[5,12,32,257]{3,2,1,0:T(8,128)S(1)} %fusion.109), kind=kOutput, calls=%fused_computation.443 | output fusion | flops 1974016 | bytes 3955200 | tf_op jit(solution)/shard_map/sub | solution.py:165
  310.9 62.6 %all-gather.29.cloned.1.call-done = bf16[768,3072]{1,0:T(8,128)(2,1)} async-done(((bf16[24,3072]{1,0:T(8,128)(2,1)}), bf16[768,3072]{1,0:T(8,128)(2,1)}) %all-gather.29.cloned.1.call-update) | async-done | bytes 4718608 | tf_op jit(solution)/shard_map/all_gather | solution.py:151
  373.5 6.5 fusion.49
  382.6 14.4 %multiply_convert_fusion.1 = (bf16[5,96,3072]{2,1,0:T(8,128)(2,1)}, f32[5,96,3072]{2,1,0:T(8,128)}) fusion(f32[5,96,3072]{2,1,0:T(8,128)S(1)} %get-tuple-element.98, f32[3072]{0:T(1024)S(1)} %reshape.588, u8[96,3072]{1,0:T(8,128)(4,1)S(1)} %get-tuple-element.25, u8[96,3072]{1,0:T(8,128)(4,1)S(1)} %get-tuple-element.24), kind=kLoop, calls=%fused_computation.12 | loop fusion | flops 104693760 | bytes 15347712 | tf_op jit(solution)/shard_map/convert_element_type | solution.py:331
  397.0 41.4 %all-gather.31.cloned.1.call-done = bf16[3072,768]{1,0:T(8,128)(2,1)} async-done(((bf16[96,768]{1,0:T(8,128)(2,1)}), bf16[3072,768]{1,0:T(8,128)(2,1)}) %all-gather.31.cloned.1.call-update) | async-done | bytes 4718608 | tf_op jit(solution)/shard_map/all_gather | solution.py:151
  452.3 67.6 %all-gather.10 = bf16[32,15,256]{2,1,0:T(8,128)(2,1)S(1)} all-gather(bf16[1,15,256]{2,1,0:T(8,128)(2,1)S(1)} %maximum_bitcast_fusion), channel_id=3, replica_groups=mesh['rep'=4,'fsdp'=8] {'rep','fsdp'}, dimensions={0}, use_global_device_ids=true | all-gather | bytes 253440 | tf_op jit(solution)/shard_map/all_gather | solution.py:345
  542.9 9.6 convert_reduce_fusion
  649.3 6.7 fusion.23
  657.9 37.7 %all-reduce.3 = (f32[2304]{0:T(1024)S(1)}, f32[8192]{0:T(1024)S(1)}) all-reduce(f32[2304]{0:T(1024)S(1)} %pad_maximum_fusion.4, f32[8192]{0:T(1024)S(1)} %constant_dynamic-update-slice_fusion.6), channel_id=1, replica_groups=mesh['rep'=4,'fsdp'=8] {'rep','fsdp'}, use_global_device_ids=true, to_apply=%region_33.34 | all-reduce | flops 10496 | bytes 83968 | tf_op jit(solution)/shard_map/psum | solution.py:458
  731.0 7.1 collective-permute-done.37
  756.6 8.6 collective-permute-done.21
  841.2 6.9 collective-permute-done.1
  855.4 40.6 %collective-permute-done.2 = bf16[2,2,48,1152]{3,2,1,0:T(8,128)(2,1)S(1)} collective-permute-done((bf16[2,2,48,1152]{3,2,1,0:T(8,128)(2,1)S(1)}, bf16[2,2,48,1152]{3,2,1,0:T(8,128)(2,1)S(1)}, u32[]{:S(2)}, u32[]{:S(2)}) %collective-permute-start.2) | collective-permute-done | bytes 442400 | tf_op jit(solution)/shard_map/ppermute | solution.py:89
  909.3 7.0 all-gather.2
  937.5 7.0 all-gather.5
  950.3 10.0 %collective-permute-done.29 = bf16[48,1536]{1,0:T(8,128)(2,1)S(1)} collective-permute-done((bf16[48,1536]{1,0:T(8,128)(2,1)S(1)}, bf16[48,1536]{1,0:T(8,128)(2,1)S(1)}, u32[]{:S(2)}, u32[]{:S(2)}) %collective-permute-start.29) | collective-permute-done | bytes 147488 | tf_op jit(solution)/shard_map/ppermute | solution.py:89
  960.4 7.0 all-gather.7
  969.3 7.8 all-gather.8
  (650 shorter events, 414.0 us)
Async XLA Ops:
  7.2 153.0 %all-gather.19.cloned.1.call-start = ((), (), s32[]{:S(2)}) async-start(), calls=%async_computation | async-start | bytes 3649536 | tf_op jit(solution)/shard_map/all_gather | solution.py:151
  8.9 163.7 %all-gather.21.cloned.1.call-start = ((), (), s32[]{:S(2)}) async-start(), calls=%async_computation.1 | async-start | bytes 1216512 | tf_op jit(solution)/shard_map/all_gather | solution.py:151
  10.4 177.5 %all-gather.25.cloned.1.call-start = ((), (), s32[]{:S(2)}) async-start(), calls=%async_computation.3 | async-start | bytes 1216512 | tf_op jit(solution)/shard_map/all_gather | solution.py:151
  11.9 240.3 %all-gather.23.cloned.1.call-start = ((), (), s32[]{:S(2)}) async-start(), calls=%async_computation.2 | async-start | bytes 4460544 | tf_op jit(solution)/shard_map/all_gather | solution.py:158
  13.5 294.2 %all-gather.27.cloned.1.call-start = ((), (), s32[]{:S(2)}) async-start(), calls=%async_computation.4 | async-start | bytes 1216512 | tf_op jit(solution)/shard_map/all_gather | solution.py:151
  15.0 358.6 %all-gather.29.cloned.1.call-start = ((), (), s32[]{:S(2)}) async-start(), calls=%async_computation.5 | async-start | bytes 4866048 | tf_op jit(solution)/shard_map/all_gather | solution.py:151
  15.7 422.6 %all-gather.31.cloned.1.call-start = ((), (), s32[]{:S(2)}) async-start(), calls=%async_computation.6 | async-start | bytes 4866048 | tf_op jit(solution)/shard_map/all_gather | solution.py:151
  620.0 200.7 %collective-permute-start = (bf16[768,1152]{1,0:T(8,128)(2,1)}, bf16[768,1152]{1,0:T(8,128)(2,1)}, u32[]{:S(2)}, u32[]{:S(2)}) collective-permute-start(bf16[768,1152]{1,0:T(8,128)(2,1)} %fusion.22), channel_id=1, source_target_pairs={{0,8},{8,0},{16,24},{24,16},{1,9},{9,1},{17,25},{25,17},{2,10},{10... | collective-permute-start | bytes 5308424 | tf_op jit(solution)/shard_map/ppermute | solution.py:89
  621.4 103.3 %collective-permute-start.5 = (bf16[768,384]{1,0:T(8,128)(2,1)}, bf16[768,384]{1,0:T(8,128)(2,1)}, u32[]{:S(2)}, u32[]{:S(2)}) collective-permute-start(bf16[768,384]{1,0:T(8,128)(2,1)} %convolution_convert_fusion.20), channel_id=1, source_target_pairs={{0,8},{8,0},{16,24},{24,16},{1,9},{9,1},{17,25},{25,17},{2,10},{10... | collective-permute-start | bytes 1769480 | tf_op jit(solution)/shard_map/ppermute | solution.py:89
  623.1 103.8 %collective-permute-start.10 = (bf16[768,384]{1,0:T(8,128)(2,1)}, bf16[768,384]{1,0:T(8,128)(2,1)}, u32[]{:S(2)}, u32[]{:S(2)}) collective-permute-start(bf16[768,384]{1,0:T(8,128)(2,1)} %convolution_convert_fusion.18), channel_id=1, source_target_pairs={{0,8},{8,0},{16,24},{24,16},{1,9},{9,1},{17,25},{25,17},{2,10},{10... | collective-permute-start | bytes 1769480 | tf_op jit(solution)/shard_map/ppermute | solution.py:89
  656.0 170.2 %collective-permute-start.15 = (bf16[1408,768]{0,1:T(8,128)(2,1)}, bf16[1408,768]{0,1:T(8,128)(2,1)}, u32[]{:S(2)}, u32[]{:S(2)}) collective-permute-start(bf16[1408,768]{0,1:T(8,128)(2,1)} %fusion.23), channel_id=1, source_target_pairs={{0,8},{8,0},{16,24},{24,16},{1,9},{9,1},{17,25},{25,17},{2,10},{10... | collective-permute-start | bytes 6488072 | tf_op jit(solution)/shard_map/ppermute | solution.py:89
  657.7 57.0 %collective-permute-start.35 = (bf16[768,256]{0,1:T(8,128)(2,1)}, bf16[768,256]{0,1:T(8,128)(2,1)}, u32[]{:S(2)}, u32[]{:S(2)}) collective-permute-start(bf16[768,256]{0,1:T(8,128)(2,1)} %fusion.95), channel_id=1, source_target_pairs={{0,8},{8,0},{16,24},{24,16},{1,9},{9,1},{17,25},{25,17},{2,10},{10... | collective-permute-start | bytes 1179656 | tf_op jit(solution)/shard_map/ppermute | solution.py:89
  724.7 112.5 %collective-permute-start.25 = (bf16[768,1536]{1,0:T(8,128)(2,1)}, bf16[768,1536]{1,0:T(8,128)(2,1)}, u32[]{:S(2)}, u32[]{:S(2)}) collective-permute-start(bf16[768,1536]{1,0:T(8,128)(2,1)} %convolution_convert_fusion.5), channel_id=1, source_target_pairs={{0,8},{8,0},{16,24},{24,16},{1,9},{9,1},{17,25},{25,17},{2,10},{10... | collective-permute-start | bytes 7077896 | tf_op jit(solution)/shard_map/ppermute | solution.py:89
  726.9 29.0 %collective-permute-start.6 = (bf16[2,2,2,48,384]{4,3,2,1,0:T(8,128)(2,1)S(1)}, bf16[2,2,2,48,384]{4,3,2,1,0:T(8,128)(2,1)S(1)}, u32[]{:S(2)}, u32[]{:S(2)}) collective-permute-start(bf16[2,2,2,48,384]{4,3,2,1,0:T(8,128)(2,1)S(1)} %dynamic-slice_bitcast_fusion.12), channel_id=1, source_target_pairs={{0,16},{8,24},{16,0},{24,8},{1,17},{9,25},{17,1},{25,9},{2,18},{10... | collective-permute-start | bytes 884744 | tf_op jit(solution)/shard_map/ppermute | solution.py:89
  756.3 94.5 %collective-permute-start.30 = (bf16[3072,384]{1,0:T(8,128)(2,1)}, bf16[3072,384]{1,0:T(8,128)(2,1)}, u32[]{:S(2)}, u32[]{:S(2)}) collective-permute-start(bf16[3072,384]{1,0:T(8,128)(2,1)} %convolution_convert_fusion.1), channel_id=1, source_target_pairs={{0,8},{8,0},{16,24},{24,16},{1,9},{9,1},{17,25},{25,17},{2,10},{10... | collective-permute-start | bytes 7077896 | tf_op jit(solution)/shard_map/ppermute | solution.py:89
  825.8 22.2 %collective-permute-start.1 = (bf16[2,2,2,48,1152]{4,3,2,1,0:T(8,128)(2,1)}, bf16[2,2,2,48,1152]{4,3,2,1,0:T(8,128)(2,1)}, u32[]{:S(2)}, u32[]{:S(2)}) collective-permute-start(bf16[2,2,2,48,1152]{4,3,2,1,0:T(8,128)(2,1)} %dynamic-slice_bitcast_fusion.3), channel_id=1, source_target_pairs={{0,1},{1,0},{2,3},{3,2},{4,5},{5,4},{6,7},{7,6},{8,9},{9,8},{10,11... | collective-permute-start | bytes 2654216 | tf_op jit(solution)/shard_map/ppermute | solution.py:89
  835.4 63.3 %collective-permute-start.16 = (bf16[2,2,2,88,768]{4,3,2,1,0:T(8,128)(2,1)S(1)}, bf16[2,2,2,88,768]{4,3,2,1,0:T(8,128)(2,1)S(1)}, u32[]{:S(2)}, u32[]{:S(2)}) collective-permute-start(bf16[2,2,2,88,768]{4,3,2,1,0:T(8,128)(2,1)S(1)} %dynamic-slice_bitcast_fusion.2), channel_id=1, source_target_pairs={{0,16},{8,24},{16,0},{24,8},{1,17},{9,25},{17,1},{25,9},{2,18},{10... | collective-permute-start | bytes 3244040 | tf_op jit(solution)/shard_map/ppermute | solution.py:89
  840.8 76.8 %collective-permute-start.26 = (bf16[2,2,2,48,1536]{4,3,2,1,0:T(8,128)(2,1)S(1)}, bf16[2,2,2,48,1536]{4,3,2,1,0:T(8,128)(2,1)S(1)}, u32[]{:S(2)}, u32[]{:S(2)}) collective-permute-start(bf16[2,2,2,48,1536]{4,3,2,1,0:T(8,128)(2,1)S(1)} %dynamic-slice_bitcast_fusion.1), channel_id=1, source_target_pairs={{0,16},{8,24},{16,0},{24,8},{1,17},{9,25},{17,1},{25,9},{2,18},{10... | collective-permute-start | bytes 3538952 | tf_op jit(solution)/shard_map/ppermute | solution.py:89
  849.5 46.5 %collective-permute-start.2 = (bf16[2,2,48,1152]{3,2,1,0:T(8,128)(2,1)S(1)}, bf16[2,2,48,1152]{3,2,1,0:T(8,128)(2,1)S(1)}, u32[]{:S(2)}, u32[]{:S(2)}) collective-permute-start(bf16[2,2,48,1152]{3,2,1,0:T(8,128)(2,1)S(1)} %dynamic-slice_bitcast_fusion.7), channel_id=1, source_target_pairs={{0,16},{8,24},{16,0},{24,8},{1,17},{9,25},{17,1},{25,9},{2,18},{10... | collective-permute-start | bytes 1327112 | tf_op jit(solution)/shard_map/ppermute | solution.py:89
  854.6 66.8 %collective-permute-start.31 = (bf16[2,2,2,192,384]{4,3,2,1,0:T(8,128)(2,1)S(1)}, bf16[2,2,2,192,384]{4,3,2,1,0:T(8,128)(2,1)S(1)}, u32[]{:S(2)}, u32[]{:S(2)}) collective-permute-start(bf16[2,2,2,192,384]{4,3,2,1,0:T(8,128)(2,1)S(1)} %dynamic-slice_bitcast_fusion), channel_id=1, source_target_pairs={{0,1},{1,0},{2,3},{3,2},{4,5},{5,4},{6,7},{7,6},{8,9},{9,8},{10,11... | collective-permute-start | bytes 3538952 | tf_op jit(solution)/shard_map/ppermute | solution.py:89
  905.1 14.3 %collective-permute-start.17 = (bf16[2,2,88,768]{3,2,1,0:T(8,128)(2,1)S(1)}, bf16[2,2,88,768]{3,2,1,0:T(8,128)(2,1)S(1)}, u32[]{:S(2)}, u32[]{:S(2)}) collective-permute-start(bf16[2,2,88,768]{3,2,1,0:T(8,128)(2,1)S(1)} %dynamic-slice_bitcast_fusion.6), channel_id=1, source_target_pairs={{0,1},{1,0},{2,3},{3,2},{4,5},{5,4},{6,7},{7,6},{8,9},{9,8},{10,11... | collective-permute-start | bytes 1622024 | tf_op jit(solution)/shard_map/ppermute | solution.py:89
  918.0 15.6 %collective-permute-start.27 = (bf16[2,2,48,1536]{3,2,1,0:T(8,128)(2,1)S(1)}, bf16[2,2,48,1536]{3,2,1,0:T(8,128)(2,1)S(1)}, u32[]{:S(2)}, u32[]{:S(2)}) collective-permute-start(bf16[2,2,48,1536]{3,2,1,0:T(8,128)(2,1)S(1)} %dynamic-slice_bitcast_fusion.5), channel_id=1, source_target_pairs={{0,1},{1,0},{2,3},{3,2},{4,5},{5,4},{6,7},{7,6},{8,9},{9,8},{10,11... | collective-permute-start | bytes 1769480 | tf_op jit(solution)/shard_map/ppermute | solution.py:89
  921.8 15.1 %collective-permute-start.32 = (bf16[2,2,192,384]{3,2,1,0:T(8,128)(2,1)S(1)}, bf16[2,2,192,384]{3,2,1,0:T(8,128)(2,1)S(1)}, u32[]{:S(2)}, u32[]{:S(2)}) collective-permute-start(bf16[2,2,192,384]{3,2,1,0:T(8,128)(2,1)S(1)} %dynamic-slice_bitcast_fusion.4), channel_id=1, source_target_pairs={{0,16},{8,24},{16,0},{24,8},{1,17},{9,25},{17,1},{25,9},{2,18},{10... | collective-permute-start | bytes 1769480 | tf_op jit(solution)/shard_map/ppermute | solution.py:89
  949.5 19.7 %collective-permute-start.34 = (bf16[192,384]{1,0:T(8,128)(2,1)S(1)}, bf16[192,384]{1,0:T(8,128)(2,1)S(1)}, u32[]{:S(2)}, u32[]{:S(2)}) collective-permute-start(bf16[192,384]{1,0:T(8,128)(2,1)S(1)} %dynamic-slice_bitcast_fusion.16), channel_id=1, source_target_pairs={{0,4},{1,5},{2,6},{3,7},{4,0},{5,1},{6,2},{7,3},{8,12},{9,13},{10,... | collective-permute-start | bytes 442376 | tf_op jit(solution)/shard_map/ppermute | solution.py:89
  (155 other events, 2647.7 us)
Sparse Core Ops, SparseCore 0:
  11.5 62.9 all-gather.18
  78.0 53.4 all-gather.20
  135.0 52.8 all-gather.24
  191.2 60.9 all-gather.22
  254.9 52.7 all-gather.26
  311.0 62.4 all-gather.28
  376.4 61.9 all-gather.30

commit v2 on v1

--- a/solution.py
+++ b/solution.py
@@ -105,44 +105,110 @@
     return rep + fsdp if first == "rep" else fsdp[:1] + rep + fsdp[1:]
 
 
-def shard_sum(values, gradient, first):
+def add(left, right):
+    return (left.astype(jnp.float32) + right.astype(jnp.float32)).astype(jnp.bfloat16)
+
+
+class Flow:
+    def __init__(self, sent, kept, first):
+        self.kept = kept
+        self.got = swap(sent, "rep", 1)
+        self.left = route(first)
+        fsdp = [("fsdp", step) for step in reversed(bits("fsdp"))]
+        rep = [("rep", step) for step in reversed(bits("rep")[1:])]
+        self.places = fsdp + rep
+        rows = kept.shape[0] // 2 ** len(self.places)
+        self.shape = (2,) * len(self.places) + (rows, kept.shape[1])
+
+    def advance(self):
+        if self.got is None:
+            return
+        total = add(self.kept, self.got)
+        if self.shape is not None:
+            total = total.reshape(self.shape)
+            self.shape = None
+        self.kept, self.got = total, None
+        if self.left:
+            (axis, step), self.left = self.left[0], self.left[1:]
+            at = self.places.index((axis, step))
+            self.places = self.places[:at] + self.places[at + 1 :]
+            here = bit_of(axis, step)
+            away = lax.dynamic_index_in_dim(total, 1 - here, at, False)
+            self.kept = lax.dynamic_index_in_dim(total, here, at, False)
+            self.got = swap(away, axis, step)
+
+    def shard(self):
+        whole = self.kept
+        for step in bits("rep")[1:]:
+            whole = join(whole, 0, "rep", step)
+        whole = whole.reshape(-1, whole.shape[-1])
+        return join(whole, 1, "rep", 1).reshape(whole.shape[0], -1).astype(jnp.float32)
+
+
+def tie(value, *flows):
+    flows = [flow for flow in flows if flow.got is not None]
+    tied = lax.optimization_barrier((value, *[flow.got for flow in flows]))
+    for flow, got in zip(flows, tied[1:]):
+        flow.got = got
+        flow.advance()
+    return tied[0]
+
+
+def gradient_halves(values, gradient):
     flat_values = values.reshape(-1, values.shape[-1])
     flat_gradient = gradient.reshape(-1, gradient.shape[-1])
     half = flat_gradient.shape[1] // 2
     core = bit_of("rep", 1)
     other = lax.dynamic_slice_in_dim(flat_gradient, (1 - core) * half, half, 1)
     mine = lax.dynamic_slice_in_dim(flat_gradient, core * half, half, 1)
-    sent = outer_sum(flat_values, other).astype(jnp.bfloat16)
-    kept = outer_sum(flat_values, mine).astype(jnp.bfloat16)
-    return halves(sent, kept, first)
-
-
-def halves(sent, kept, first):
-    total = add(kept, swap(sent, "rep", 1))
-    fsdp = [("fsdp", step) for step in reversed(bits("fsdp"))]
-    rep = [("rep", step) for step in reversed(bits("rep")[1:])]
-    places = fsdp + rep
-    rows = total.shape[0] // 2 ** len(places)
-    total = total.reshape((2,) * len(places) + (rows, total.shape[1]))
-    for axis, step in route(first):
-        at = places.index((axis, step))
-        here = bit_of(axis, step)
-        away = lax.dynamic_index_in_dim(total, 1 - here, at, False)
-        stay = lax.dynamic_index_in_dim(total, here, at, False)
-        total = add(stay, swap(away, axis, step))
-        places = places[:at] + places[at + 1 :]
-    return total
-
-
-def add(left, right):
-    return (left.astype(jnp.float32) + right.astype(jnp.float32)).astype(jnp.bfloat16)
-
-
-def whole_shard(piece):
-    every = lax.all_gather(piece, "rep", axis=0, tiled=False)
-    rows, columns = piece.shape
-    every = every.reshape(-1, 2, rows, columns).transpose(0, 2, 1, 3)
-    return every.reshape(-1, 2 * columns).astype(jnp.float32)
+    return (
+        outer_sum(flat_values, other).astype(jnp.bfloat16),
+        outer_sum(flat_values, mine).astype(jnp.bfloat16),
+    )
+
+
+def blocks_of(shard, widths):
+    half = shard.shape[1] // 2
+    blocks = []
+    start = 0
+    for width in widths:
+        size = width // 2
+        pair = [shard[:, at + start : at + start + size] for at in (0, half)]
+        blocks.append(jnp.concatenate(pair, axis=1))
+        start += size
+    return blocks
+
+
+def side_by_side(*pairs):
+    return tuple(jnp.concatenate(blocks, axis=1) for blocks in zip(*pairs))
+
+
+def join(values, at, axis, step):
+    theirs = swap(values, axis, step)
+    first = bit_of(axis, step) == 0
+    return jnp.stack([jnp.where(first, values, theirs), jnp.where(first, theirs, values)], axis=at)
+
+
+def join_fsdp(values):
+    for step in bits("fsdp"):
+        values = join(values, 0, "fsdp", step)
+        values = values.reshape(-1, *values.shape[2:])
+    return values
+
+
+def join_all(values):
+    values = join_fsdp(values)
+    for step in bits("rep"):
+        values = join(values, 0, "rep", step)
+        values = values.reshape(-1, *values.shape[2:])
+    return values
+
+
+def sum_everywhere(values):
+    for axis in ("rep", "fsdp"):
+        for step in bits(axis):
+            values = values + swap(values, axis, step)
+    return values
 
 
 def gather_rows(shard):
@@ -151,12 +217,53 @@
     return lax.all_gather(mine, ("fsdp", "rep"), axis=0, tiled=True)
 
 
-def gather_columns(shard):
+def part_of(shard, count, at, axis):
+    size = shard.shape[axis] // count
+    return lax.dynamic_slice_in_dim(shard, at * size, size, axis)
+
+
+def exchange_rows(shard, first):
     count = lax.axis_size("rep")
-    part = shard.shape[1] // count
-    mine = lax.dynamic_slice_in_dim(shard, lax.axis_index("rep") * part, part, 1)
-    whole = lax.all_gather(mine, ("rep", "fsdp"), axis=0, tiled=True)
-    return whole.reshape(count, -1, part)
+    mine = part_of(shard, count, lax.axis_index("rep"), 0)
+    rows, columns = mine.shape
+    whole = mine[None]
+    fsdp, rep = bits("fsdp"), bits("rep")
+    for step in fsdp[1:]:
+        whole = join(whole, 0, "fsdp", step).reshape(-1, rows, columns)
+    if first == "rep":
+        whole = whole[:, None]
+        for step in rep[1:]:
+            whole = join(whole, 1, "rep", step).reshape(whole.shape[0], -1, rows, columns)
+        whole = join(whole, 1, "fsdp", 1)
+    else:
+        whole = join(whole, 1, "fsdp", 1)[:, :, None]
+        for step in rep[1:]:
+            whole = join(whole, 2, "rep", step).reshape(*whole.shape[:2], -1, rows, columns)
+    whole = join(whole, 3, "rep", 1)
+    return whole.reshape(-1, columns)
+
+
+def exchange_columns(shard, first):
+    fsdp, rep = bits("fsdp"), bits("rep")
+    mine = part_of(shard, 2, bit_of("rep", 1), 1)
+    mine = part_of(mine, 2 ** len(rep[1:]), lax.axis_index("rep") // 2, 0)
+    rows, columns = mine.shape
+    whole = mine[None]
+    for step in fsdp[1:]:
+        whole = join(whole, 0, "fsdp", step).reshape(-1, rows, columns)
+    if first == "rep":
+        whole = whole[:, None]
+        for step in rep[1:]:
+            whole = join(whole, 1, "rep", step).reshape(whole.shape[0], -1, rows, columns)
+        whole = join(whole, 1, "fsdp", 1)
+    else:
+        whole = join(whole, 1, "fsdp", 1)[:, :, None]
+        for step in rep[1:]:
+            whole = join(whole, 2, "rep", step).reshape(*whole.shape[:2], -1, rows, columns)
+    whole = whole.reshape(-1, columns)
+    theirs = swap(whole, "rep", 1)
+    core = bit_of("rep", 1) == 0
+    return (jnp.where(core, whole, theirs), jnp.where(core, theirs, whole))
 
 
 def attend(queries, key_rows, value_rows, allowed):
@@ -272,7 +379,7 @@
         picture_vector_offset,
         sentence_vector_offset,
     )
-    packed = lax.all_gather(jnp.concatenate(vectors), "fsdp", axis=0, tiled=False)
+    packed = join_fsdp(jnp.concatenate(vectors)[None])
     spread = []
     offset = 0
     for vector in vectors:
@@ -293,19 +400,28 @@
         image_shift,
         text_shift,
     ) = spread
-    owners = lax.all_gather(sentence_picture_owner, everywhere, axis=0, tiled=True)
-
-    w_qkv = gather_rows(attend_triple_matrix)
-    w_self_out = gather_rows(inward_result_matrix)
-    w_keyval = gather_columns(visual_lookup_pairs)
-    w_asker = gather_rows(mixing_asker_matrix)
-    w_cross_out = gather_rows(mixing_result_matrix)
-    w_up = gather_rows(widening_matrix)
-    w_down = gather_rows(narrowing_matrix)
-    w_ends = gather_rows(jnp.concatenate([picture_mapping_matrix, sentence_mapping_matrix], axis=1))
+    owners = join_all(sentence_picture_owner[None]).reshape(-1)
+
     emb = picture_mapping_matrix.shape[1]
-    w_image = w_ends[:, :emb]
-    w_text = w_ends[:, emb:]
+    w_self = gather_rows(jnp.concatenate([attend_triple_matrix, inward_result_matrix], axis=1))
+    w_qkv, w_self_out = w_self[:, : 3 * width], w_self[:, 3 * width :]
+    w_keys, w_values = exchange_columns(visual_lookup_pairs, "rep")
+    w_rest = gather_rows(
+        jnp.concatenate(
+            [
+                mixing_asker_matrix,
+                mixing_result_matrix,
+                widening_matrix,
+                picture_mapping_matrix,
+                sentence_mapping_matrix,
+            ],
+            axis=1,
+        )
+    )
+    w_asker, w_cross_out = w_rest[:, :width], w_rest[:, width : 2 * width]
+    w_up = w_rest[:, 2 * width : -2 * emb]
+    w_image, w_text = w_rest[:, -2 * emb : -emb], w_rest[:, -emb:]
+    w_down = exchange_rows(narrowing_matrix, "fsdp")
 
     qkv = project(sequence_entries, w_qkv).astype(bf16)
     q_self, k_self, v_self = (qkv[..., i * width : (i + 1) * width] for i in range(3))
@@ -316,11 +432,8 @@
     head_rows = inner[:, :QUERY]
     head_low = head_rows.astype(bf16)
     asked = project(head_low, w_asker).astype(bf16)
-    parts = w_keyval.shape[0]
-    keyval = jnp.concatenate(
-        [project(picture_descriptors, w_keyval[i]).astype(bf16) for i in range(parts)], axis=-1
-    )
-    k_cross, v_cross = keyval[..., :width], keyval[..., width:]
+    k_cross = project(picture_descriptors, w_keys).astype(bf16)
+    v_cross = project(picture_descriptors, w_values).astype(bf16)
     cross_mix, cross_probs = attend(asked, k_cross, v_cross, None)
     second_sum = head_rows + project(cross_mix, w_cross_out) + cross_offset
     normed = layer_norm(second_sum, cross_scale, cross_shift)
@@ -342,9 +455,7 @@
     caption_low = caption_low.astype(bf16).reshape(-1, width)
     text_raw = project(caption_low, w_text) + text_shift
     text_unit = unit_rows(text_raw).astype(bf16)
-    units = lax.all_gather(
-        jnp.concatenate([image_unit, text_unit], axis=0), everywhere, axis=0, tiled=False
-    )
+    units = join_all(jnp.concatenate([image_unit, text_unit], axis=0)[None])
     all_images = units[:, :rows].reshape(-1, emb)
     all_texts = units[:, rows:].reshape(-1, emb)
     image_total = all_images.shape[0]
@@ -400,46 +511,63 @@
         third_sum, feed_scale, feed_shift, grad_final
     )
     grad_third = grad_third_sum.astype(bf16)
-    down_piece = shard_sum(activated, grad_third, "fsdp")
+    down = Flow(*gradient_halves(activated, grad_third), "fsdp")
     grad_active = project_back(grad_third, w_down)
     _, gelu_pull = jax.vjp(exact_gelu, pre_act)
     grad_pre = gelu_pull(grad_active)[0].astype(bf16)
-    up_piece = shard_sum(merged_low, grad_pre, "rep")
-    grad_merged = grad_third_sum + project_back(grad_pre, w_up)
+    grad_pre = tie(grad_pre, down)
     ends = jnp.concatenate(
         [outer_sum(pooled_low, grad_image_raw), outer_sum(caption_low, grad_text_raw)], axis=1
     ).astype(bf16)
-    core = bit_of("rep", 1)
-    ends_sent = lax.dynamic_slice_in_dim(ends, (1 - core) * emb, emb, 1)
-    ends_kept = lax.dynamic_slice_in_dim(ends, core * emb, emb, 1)
-    ends_piece = halves(ends_sent, ends_kept, "fsdp")
+    ends_halves = (part_of(ends, 2, 1 - bit_of("rep", 1), 1), part_of(ends, 2, bit_of("rep", 1), 1))
+    up = Flow(*side_by_side(gradient_halves(merged_low, grad_pre), ends_halves), "rep")
+    grad_merged = grad_third_sum + project_back(grad_pre, w_up)
+    grad_merged = tie(grad_merged, up)
 
     grad_second_sum, cross_gain, cross_shift_grad = norm_back(
         second_sum, cross_scale, cross_shift, grad_merged[:, :QUERY]
     )
     grad_second = grad_second_sum.astype(bf16)
     grad_cross_mix = project_back(grad_second, w_cross_out).astype(bf16)
-    cross_out_piece = shard_sum(cross_mix, grad_second, "fsdp")
+    cross_out_halves = gradient_halves(cross_mix, grad_second)
     grad_asked, grad_key, grad_value = attend_back(
         asked, k_cross, v_cross, cross_probs, grad_cross_mix
     )
     grad_asked = grad_asked.astype(bf16)
-    grad_keyval = jnp.concatenate([grad_key, grad_value], axis=-1).astype(bf16)
-    keyval_piece = shard_sum(picture_descriptors, grad_keyval, "rep")
-    asker_piece = shard_sum(head_low, grad_asked, "fsdp")
+    grad_asked = tie(grad_asked, down, up)
+    core_zero = bit_of("rep", 1) == 0
+    grad_key = grad_key.astype(bf16)
+    grad_value = grad_value.astype(bf16)
+    keyval = Flow(
+        outer_sum(picture_descriptors, jnp.where(core_zero, grad_value, grad_key)).astype(bf16),
+        outer_sum(picture_descriptors, jnp.where(core_zero, grad_key, grad_value)).astype(bf16),
+        "fsdp",
+    )
+    asker_halves = gradient_halves(head_low, grad_asked)
     grad_head = grad_second_sum + project_back(grad_asked, w_asker)
     grad_inner = jnp.concatenate([grad_head, grad_merged[:, QUERY:]], axis=1)
+    grad_inner = tie(grad_inner, down, keyval)
 
     grad_first_sum, self_gain, self_shift_grad = norm_back(
         first_sum, self_scale, self_shift, grad_inner
     )
     grad_first = grad_first_sum.astype(bf16)
-    self_out_piece = shard_sum(self_mix, grad_first, "rep")
+    middle = Flow(
+        *side_by_side(cross_out_halves, asker_halves, gradient_halves(self_mix, grad_first)), "rep"
+    )
     grad_self_mix = project_back(grad_first, w_self_out).astype(bf16)
+    grad_self_mix = tie(grad_self_mix, up, middle)
     grad_q, grad_k, grad_v = attend_back(q_self, k_self, v_self, self_probs, grad_self_mix)
     grad_qkv = jnp.concatenate([grad_q, grad_k, grad_v], axis=-1).astype(bf16)
-    qkv_piece = shard_sum(sequence_entries, grad_qkv, "fsdp")
+    grad_qkv = tie(grad_qkv, down, up, keyval)
+    cut = 4 * grad_qkv.shape[-1] // 9
+    left = Flow(*gradient_halves(sequence_entries, grad_qkv[..., :cut]), "rep")
+    right = Flow(*gradient_halves(sequence_entries, grad_qkv[..., cut:]), "fsdp")
+    flows = (down, up, keyval, middle, left, right)
     incoming = grad_first_sum + project_back(grad_qkv, w_qkv)
+    while any(flow.got is not None for flow in flows):
+        for flow in flows:
+            flow.advance()
 
     early = (
         column_sum(grad_pre),
@@ -455,7 +583,7 @@
     late = (column_sum(grad_first), self_gain, self_shift_grad)
     shards = []
     for group in (early, late):
-        summed = lax.psum(jnp.concatenate(group), everywhere)
+        summed = sum_everywhere(jnp.concatenate(group)[None])[0]
         offset = 0
         for vector in group:
             size = vector.shape[0]
@@ -477,30 +605,34 @@
         self_gain,
         self_shift_grad,
     ) = shards
-    ends_shard = whole_shard(ends_piece)
+    up_shard, middle_shard = up.shard(), middle.shard()
+    inner_width = up_bias.shape[0] * lax.axis_size("fsdp")
+    up_grad, ends_grad = blocks_of(up_shard, (inner_width, 2 * emb))
+    cross_out_grad, asker_grad, self_out_grad = blocks_of(middle_shard, (width,) * 3)
+    qkv_grad = jnp.concatenate([left.shard(), right.shard()], axis=1)
     return (
         out,
         incoming,
-        whole_shard(qkv_piece),
-        whole_shard(self_out_piece),
+        qkv_grad,
+        self_out_grad,
         self_bias,
         self_gain,
         self_shift_grad,
-        whole_shard(asker_piece),
-        whole_shard(keyval_piece),
-        whole_shard(cross_out_piece),
+        asker_grad,
+        keyval.shard(),
+        cross_out_grad,
         cross_bias,
         cross_gain,
         cross_shift_grad,
-        whole_shard(up_piece),
+        up_grad,
         up_bias,
-        whole_shard(down_piece),
+        down.shard(),
         down_bias,
         feed_gain,
         feed_shift_grad,
-        ends_shard[:, :emb],
+        ends_grad[:, :emb],
         image_bias,
-        ends_shard[:, emb:],
+        ends_grad[:, emb:],
         text_bias,
         sharpness_adjoint,
     )

time: 992 us -> 592 us (0.60)
  blocking collectives: 275 us -> 0 us
  waiting for transfers between devices: 298 us -> 181 us
  local copies, waits for them, and re-layouts: 141 us -> 85.6 us
  other arithmetic: 58.2 us -> 92.8 us
  starting transfers between devices: 48.3 us -> 71.7 us
  matrix products: 145 us -> 131 us
    all_gather x10 -> x0, blocking collectives: 161 us -> none  [the longest x1 67.6 us: on_device(): lax.all_gather(jnp.concatenate([image_unit, text_unit], axis=0), everywhe...]
    all_gather x6 -> x2, waiting for transfers between devices: 121 us -> 19.7 us  [gather_rows(): return lax.all_gather(mine, ('fsdp', 'rep'), axis=0, tiled=True)]
    unnamed x2 -> x0, blocking collectives: 76.5 us -> none
    all_gather x1 -> x0, waiting for transfers between devices: 54.8 us -> none  [gather_columns(): whole = lax.all_gather(mine, ('rep', 'fsdp'), axis=0, tiled=True)]
    ppermute x40 -> x75, waiting for transfers between devices: 122 us -> 161 us  [swap(): return lax.ppermute(values, axis, [(i, i ^ step) for i in range(count)])]
    concatenate x11 -> x3, local copies, waits for them, and re-layouts: 38.5 us -> 0.11 us  [the longest x1 0.1 us: on_device(): packed = join_fsdp(jnp.concatenate(vectors)[None])]
    psum x1 -> x0, blocking collectives: 37.7 us -> none  [on_device(): summed = lax.psum(jnp.concatenate(group), everywhere)]
    ppermute x40 -> x75, starting transfers between devices: 48 us -> 71.6 us  [swap(): return lax.ppermute(values, axis, [(i, i ^ step) for i in range(count)])]
  transfers between devices with their start and end apart: 47 -> 77, of which waited for: 26 -> 35; matrix products, arithmetic and copies ran while one was open for 22% -> 46% of each run, Pallas kernels for 0% -> 0%
where the time goes in v2:
time: 592 us; the launch traced here: 583 us
  waiting for transfers between devices  181 us (31%)
  matrix products  131 us (22%)
  other arithmetic  92.8 us (16%)
  local copies, waits for them, and re-layouts  85.6 us (14%)
  starting transfers between devices  71.7 us (12%)
  between operations  21.6 us (4%)
    ppermute x75, waiting for transfers between devices, swap(): return lax.ppermute(values, axis, [(i, i ^ step) for i in range(count)])  161 us
    ppermute x75, starting transfers between devices, swap(): return lax.ppermute(values, axis, [(i, i ^ step) for i in range(count)])  71.6 us
    dot_general x20, matrix products, outer_sum(): lax.dot_general(flat_values, flat_gradient, (((0,), (0,)), ((), ())), pre...  38.5 us
    dot_general x10, matrix products, project(): jnp.einsum('...d,df->...f', values, matrix, preferred_element_type=jnp.fl...  36.3 us
    convert_element_type x28, other arithmetic, add(): (left.astype(jnp.float32) + right.astype(jnp.float32)).astype(jnp.bfloat16)  23.3 us
    dot_general x8, matrix products, project_back(): jnp.einsum('...f,df->...d', gradient, matrix, preferred_element_type=jnp....  23.1 us
    all_gather x2, waiting for transfers between devices, gather_rows(): return lax.all_gather(mine, ('fsdp', 'rep'), axis=0, tiled=True)  19.7 us
    another operation x54, other arithmetic, join(): jnp.stack([jnp.where(first, values, theirs), jnp.where(first, theirs, val...  14.9 us
  transfers between devices with their start and end apart: 77, of which 35 were waited for; matrix products, arithmetic and copies ran while one was open for 46% of the time, Pallas kernels for 0%

profile of v2, /device:TPU:0, one launch (start us, length us, event | category | flops | bytes accessed | tf_op | source)
XLA Modules:
  0.0 583.3 jit_solution(16285527244039621376)
XLA Ops:
  29.1 18.6 %collective-permute-done.4 = bf16[2,88,768]{2,1,0:T(8,128)(2,1)S(1)} collective-permute-done((bf16[2,88,768]{2,1,0:T(8,128)(2,1)S(1)}, bf16[2,88,768]{2,1,0:T(8,128)(2,1)S(1)}, u32[]{:S(2)}, u32[]{:S(2)}) %collective-permute-start.4) | collective-permute-done | bytes 270368 | tf_op jit(solution)/shard_map/ppermute | solution.py:89
  49.5 4.2 collective-permute-done.9
  55.5 9.5 %collective-permute-done.5 = bf16[4,1,88,768]{3,2,0,1:T(8,128)(2,1)S(1)} collective-permute-done((bf16[4,1,88,768]{3,2,0,1:T(8,128)(2,1)S(1)}, bf16[4,1,88,768]{3,2,0,1:T(8,128)(2,1)S(1)}, u32[]{:S(2)}, u32[]{:S(2)}) %collective-permute-start.5) | collective-permute-done | bytes 540704 | tf_op jit(solution)/shard_map/ppermute | solution.py:89
  71.9 27.8 %collective-permute-done.6 = bf16[4,2,88,768]{3,2,1,0:T(8,128)(2,1)S(1)} collective-permute-done((bf16[4,2,88,768]{3,2,1,0:T(8,128)(2,1)S(1)}, bf16[4,2,88,768]{3,2,1,0:T(8,128)(2,1)S(1)}, u32[]{:S(2)}, u32[]{:S(2)}) %collective-permute-start.6) | collective-permute-done | bytes 1081376 | tf_op jit(solution)/shard_map/ppermute | solution.py:89
  112.0 7.3 %convert_bitcast_fusion.1 = bf16[5,257,768]{2,1,0:T(8,128)(2,1)} fusion(bf16[5,257,1408]{2,1,0:T(8,128)(2,1)} %param.28, bf16[1408,768]{1,0:T(8,128)(2,1)} %collective-permute-done.7, bf16[1408,768]{1,0:T(8,128)(2,1)} %bitcast.29, pred[]{:T(512)S(6)} %eq.185), kind=kOutput, calls=%fused_computation.81 | convolution fusion | flops 2781122304 | bytes 9917697 | tf_op jit(solution)/shard_map/...d,df->...f/dot_general | solution.py:15
  119.3 4.6 copy.174
  124.0 7.3 %convert_bitcast_fusion = bf16[5,257,768]{2,1,0:T(8,128)(2,1)} fusion(bf16[5,257,1408]{2,1,0:T(8,128)(2,1)} %param.28, bf16[1408,768]{1,0:T(8,128)(2,1)} %bitcast.29, bf16[1408,768]{1,0:T(8,128)(2,1)} %collective-permute-done.7, pred[]{:T(512)S(6)} %eq.185), kind=kOutput, calls=%fused_computation.80 | convolution fusion | flops 2781122304 | bytes 9917697 | tf_op jit(solution)/shard_map/...d,df->...f/dot_general | solution.py:15
  131.3 4.4 copy.175
  157.3 19.7 %all-gather.5.cloned.1.call-done = bf16[768,5120]{1,0:T(8,128)(2,1)} async-done(((bf16[24,5120]{1,0:T(8,128)(2,1)}), bf16[768,5120]{1,0:T(8,128)(2,1)}) %all-gather.5.cloned.1.call-update) | async-done | bytes 7864336 | tf_op jit(solution)/shard_map/all_gather | solution.py:217
  182.6 10.5 %fusion.174 = (f32[5,12,32]{2,1,0:T(8,128)S(1)}, f32[5,12,32,257]{3,2,1,0:T(8,128)S(1)}) fusion(f32[5,12,32,257]{3,2,1,0:T(8,128)S(1)} %fusion.83), kind=kOutput, calls=%fused_computation.532 | output fusion | flops 1974016 | bytes 3955200 | tf_op jit(solution)/shard_map/sub | solution.py:272
  200.5 6.5 %fusion.43 = (u8[96,3072]{1,0:T(8,128)(4,1)S(1)}, u8[96,3072]{1,0:T(8,128)(4,1)S(1)}, f32[5,96,3072]{2,1,0:T(8,128)S(1)}) fusion(f32[3072]{0:T(1024)S(1)} %reshape.635, bf16[5,96,768]{2,1,0:T(8,128)(2,1)S(1)} %fusion.51, bf16[768,5120]{1,0:T(8,128)(2,1)} %all-gather.5.cloned.1.call-done), kind=kOutput, calls=%fused_computation.116 | convolution fusion | flops 2284978176 | bytes 11956224 | tf_op jit(solution)/shard_map/...d,df->...f/dot_general | solution.py:15
  207.1 14.6 %multiply_convert_fusion.1 = (bf16[5,96,3072]{2,1,0:T(8,128)(2,1)S(1)}, f32[5,96,3072]{2,1,0:T(8,128)}) fusion(f32[5,96,3072]{2,1,0:T(8,128)S(1)} %get-tuple-element.257, f32[3072]{0:T(1024)S(1)} %reshape.635, u8[96,3072]{1,0:T(8,128)(4,1)S(1)} %get-tuple-element.107, u8[96,3072]{1,0:T(8,128)(4,1)S(1)} %get-tuple-element.106), kind=kLoop, calls=%fused_computation.12 | loop fusion | flops 104693760 | bytes 15347712 | tf_op jit(solution)/shard_map/convert_element_type | solution.py:444
  289.5 3.9 convolution_convert_fusion.1
  293.5 7.9 %add_convert_fusion = bf16[5,96,3072]{2,1,0:T(8,128)(2,1)S(1)} fusion(f32[5,96,3072]{2,1,0:T(8,128)} %get-tuple-element.138, f32[5,96,3072]{2,1,0:T(8,128)S(1)} %bitcast.603, bf16[5,96,768]{2,1,0:T(8,128)(2,1)S(1)} %copy-done.59, bf16[3072,768,1]{1,0,2:T(8,128)(2,1)} %bitcast.606, f32[3072]{0:T(1024)S(1)} %copy-done.89), kind=kOutput, calls=%fused_computation.11 | convolution fusion | flops 2287042560 | bytes 20213760 | tf_op jit(solution)/shard_map/...f,df->...d/dot_general | solution.py:19
  326.8 5.3 bitcast_convert_fusion
  336.2 5.1 fusion.12
  341.3 26.3 %collective-permute-done.65 = f32[1,8192]{1,0:T(1,128)S(1)} collective-permute-done((f32[1,8192]{1,0:T(1,128)S(1)}, f32[1,8192]{1,0:T(1,128)S(1)}, u32[]{:S(2)}, u32[]{:S(2)}) %collective-permute-start.65) | collective-permute-done | bytes 32800 | tf_op jit(solution)/shard_map/ppermute | solution.py:89
  392.9 6.4 %collective-permute-done.27 = bf16[2,2,192,384]{3,2,1,0:T(8,128)(2,1)S(1)} collective-permute-done((bf16[2,2,192,384]{3,2,1,0:T(8,128)(2,1)S(1)}, bf16[2,2,192,384]{3,2,1,0:T(8,128)(2,1)S(1)}, u32[]{:S(2)}, u32[]{:S(2)}) %collective-permute-start.27) | collective-permute-done | bytes 589856 | tf_op jit(solution)/shard_map/ppermute | solution.py:89
  472.8 5.0 add_add_fusion.4
  482.2 4.6 collective-permute-done.73
  487.4 4.8 collective-permute-done.70
  531.2 6.1 %collective-permute-done.51 = bf16[48,1152]{1,0:T(8,128)(2,1)S(1)} collective-permute-done((bf16[48,1152]{1,0:T(8,128)(2,1)S(1)}, bf16[48,1152]{1,0:T(8,128)(2,1)S(1)}, u32[]{:S(2)}, u32[]{:S(2)}) %collective-permute-start.51) | collective-permute-done | bytes 110624 | tf_op jit(solution)/shard_map/ppermute | solution.py:89
  557.9 5.0 collective-permute-done.44
  564.0 4.1 collective-permute-done.45
  (758 shorter events, 342.3 us)
Async XLA Ops:
  7.4 133.0 %all-gather.3.cloned.1.call-start = ((), (), s32[]{:S(2)}) async-start(), calls=%async_computation | async-start | bytes 4866048 | tf_op jit(solution)/shard_map/all_gather | solution.py:217
  9.2 167.9 %all-gather.5.cloned.1.call-start = ((), (), s32[]{:S(2)}) async-start(), calls=%async_computation.1 | async-start | bytes 8110080 | tf_op jit(solution)/shard_map/all_gather | solution.py:217
  21.9 44.9 %collective-permute-start.14 = (s32[2,10]{1,0:T(2,128)S(1)}, s32[2,10]{1,0:T(2,128)S(1)}, u32[]{:S(2)}, u32[]{:S(2)}) collective-permute-start(s32[2,10]{1,0:T(2,128)S(1)} %bitcast.677), channel_id=1, source_target_pairs={{0,2},{1,3},{2,0},{3,1},{4,6},{5,7},{6,4},{7,5},{8,10},{9,11},{10,... | collective-permute-start | bytes 248 | tf_op jit(solution)/shard_map/ppermute | solution.py:89
  24.0 23.7 %collective-permute-start.4 = (bf16[2,88,768]{2,1,0:T(8,128)(2,1)S(1)}, bf16[2,88,768]{2,1,0:T(8,128)(2,1)S(1)}, u32[]{:S(2)}, u32[]{:S(2)}) collective-permute-start(bf16[2,88,768]{2,1,0:T(8,128)(2,1)S(1)} %maximum_bitcast_fusion.4), channel_id=1, source_target_pairs={{0,4},{1,5},{2,6},{3,7},{4,0},{5,1},{6,2},{7,3},{8,12},{9,13},{10,... | collective-permute-start | bytes 811016 | tf_op jit(solution)/shard_map/ppermute | solution.py:89
  26.8 26.9 %collective-permute-start.9 = (bf16[2,96,768]{2,1,0:T(8,128)(2,1)S(1)}, bf16[2,96,768]{2,1,0:T(8,128)(2,1)S(1)}, u32[]{:S(2)}, u32[]{:S(2)}) collective-permute-start(bf16[2,96,768]{2,1,0:T(8,128)(2,1)S(1)} %maximum_bitcast_fusion.3), channel_id=1, source_target_pairs={{0,4},{1,5},{2,6},{3,7},{4,0},{5,1},{6,2},{7,3},{8,12},{9,13},{10,... | collective-permute-start | bytes 884744 | tf_op jit(solution)/shard_map/ppermute | solution.py:89
  65.2 34.6 %collective-permute-start.6 = (bf16[4,2,88,768]{3,2,1,0:T(8,128)(2,1)S(1)}, bf16[4,2,88,768]{3,2,1,0:T(8,128)(2,1)S(1)}, u32[]{:S(2)}, u32[]{:S(2)}) collective-permute-start(bf16[4,2,88,768]{3,2,1,0:T(8,128)(2,1)S(1)} %maximum_bitcast_fusion.2), channel_id=1, source_target_pairs={{0,1},{1,0},{2,3},{3,2},{4,5},{5,4},{6,7},{7,6},{8,9},{9,8},{10,11... | collective-permute-start | bytes 3244040 | tf_op jit(solution)/shard_map/ppermute | solution.py:89
  70.2 35.9 %collective-permute-start.11 = (bf16[4,2,1,96,768]{4,3,1,0,2:T(8,128)(2,1)S(1)}, bf16[4,2,1,96,768]{4,3,1,0,2:T(8,128)(2,1)}, u32[]{:S(2)}, u32[]{:S(2)}) collective-permute-start(bf16[4,2,1,96,768]{4,3,1,0,2:T(8,128)(2,1)S(1)} %maximum_bitcast_fusion.1), channel_id=1, source_target_pairs={{0,16},{8,24},{16,0},{24,8},{1,17},{9,25},{17,1},{25,9},{2,18},{10... | collective-permute-start | bytes 3538952 | tf_op jit(solution)/shard_map/ppermute | solution.py:89
  103.3 128.1 %collective-permute-start.15 = (s32[4,10]{1,0:T(4,128)}, s32[4,10]{1,0:T(4,128)}, u32[]{:S(2)}, u32[]{:S(2)}) collective-permute-start(s32[4,10]{1,0:T(4,128)} %bitcast.66), channel_id=1, source_target_pairs={{0,4},{1,5},{2,6},{3,7},{4,0},{5,1},{6,2},{7,3},{8,12},{9,13},{10,... | collective-permute-start | bytes 488 | tf_op jit(solution)/shard_map/ppermute | solution.py:89
  109.2 26.5 %collective-permute-start.12 = (bf16[4,2,2,96,768]{4,3,2,1,0:T(8,128)(2,1)}, bf16[4,2,2,96,768]{4,3,2,1,0:T(8,128)(2,1)}, u32[]{:S(2)}, u32[]{:S(2)}) collective-permute-start(bf16[4,2,2,96,768]{4,3,2,1,0:T(8,128)(2,1)} %maximum_bitcast_fusion), channel_id=1, source_target_pairs={{0,8},{8,0},{16,24},{24,16},{1,9},{9,1},{17,25},{25,17},{2,10},{10... | collective-permute-start | bytes 7077896 | tf_op jit(solution)/shard_map/ppermute | solution.py:89
  307.3 75.1 %collective-permute-start.25 = (bf16[2,2,2,192,384]{4,3,2,1,0:T(8,128)(2,1)}, bf16[2,2,2,192,384]{4,3,2,1,0:T(8,128)(2,1)}, u32[]{:S(2)}, u32[]{:S(2)}) collective-permute-start(bf16[2,2,2,192,384]{4,3,2,1,0:T(8,128)(2,1)} %dynamic-slice_bitcast_fusion.1), channel_id=1, source_target_pairs={{0,1},{1,0},{2,3},{3,2},{4,5},{5,4},{6,7},{7,6},{8,9},{9,8},{10,11... | collective-permute-start | bytes 3538952 | tf_op jit(solution)/shard_map/ppermute | solution.py:89
  334.1 48.3 %collective-permute-start.26 = (bf16[2,2,2,48,1792]{4,3,2,1,0:T(8,128)(2,1)}, bf16[2,2,2,48,1792]{4,3,2,1,0:T(8,128)(2,1)}, u32[]{:S(2)}, u32[]{:S(2)}) collective-permute-start(bf16[2,2,2,48,1792]{4,3,2,1,0:T(8,128)(2,1)} %dynamic-slice_bitcast_fusion), channel_id=1, source_target_pairs={{0,16},{8,24},{16,0},{24,8},{1,17},{9,25},{17,1},{25,9},{2,18},{10... | collective-permute-start | bytes 4128776 | tf_op jit(solution)/shard_map/ppermute | solution.py:89
  334.7 32.9 %collective-permute-start.65 = (f32[1,8192]{1,0:T(1,128)S(1)}, f32[1,8192]{1,0:T(1,128)S(1)}, u32[]{:S(2)}, u32[]{:S(2)}) collective-permute-start(f32[1,8192]{1,0:T(1,128)S(1)} %add.696), channel_id=1, source_target_pairs={{0,16},{8,24},{16,0},{24,8},{1,17},{9,25},{17,1},{25,9},{2,18},{10... | collective-permute-start | bytes 98312 | tf_op jit(solution)/shard_map/ppermute | solution.py:89
  379.4 19.9 %collective-permute-start.28 = (bf16[1408,768]{0,1:T(8,128)(2,1)}, bf16[1408,768]{0,1:T(8,128)(2,1)S(1)}, u32[]{:S(2)}, u32[]{:S(2)}) collective-permute-start(bf16[1408,768]{0,1:T(8,128)(2,1)} %fusion.12), channel_id=1, source_target_pairs={{0,8},{8,0},{16,24},{24,16},{1,9},{9,1},{17,25},{25,17},{2,10},{10... | collective-permute-start | bytes 6488072 | tf_op jit(solution)/shard_map/ppermute | solution.py:89
  387.8 39.3 %collective-permute-start.29 = (bf16[2,2,48,1792]{3,2,1,0:T(8,128)(2,1)}, bf16[2,2,48,1792]{3,2,1,0:T(8,128)(2,1)}, u32[]{:S(2)}, u32[]{:S(2)}) collective-permute-start(bf16[2,2,48,1792]{3,2,1,0:T(8,128)(2,1)} %dynamic-slice_bitcast_fusion.4), channel_id=1, source_target_pairs={{0,1},{1,0},{2,3},{3,2},{4,5},{5,4},{6,7},{7,6},{8,9},{9,8},{10,11... | collective-permute-start | bytes 2064392 | tf_op jit(solution)/shard_map/ppermute | solution.py:89
  403.9 23.2 %collective-permute-start.30 = (bf16[768,1152]{0,1:T(8,128)(2,1)}, bf16[768,1152]{0,1:T(8,128)(2,1)}, u32[]{:S(2)}, u32[]{:S(2)}) collective-permute-start(bf16[768,1152]{0,1:T(8,128)(2,1)} %pad_maximum_fusion.4), channel_id=1, source_target_pairs={{0,8},{8,0},{16,24},{24,16},{1,9},{9,1},{17,25},{25,17},{2,10},{10... | collective-permute-start | bytes 5308424 | tf_op jit(solution)/shard_map/ppermute | solution.py:89
  413.8 47.9 %collective-permute-start.31 = (bf16[2,192,384]{2,1,0:T(8,128)(2,1)}, bf16[2,192,384]{2,1,0:T(8,128)(2,1)}, u32[]{:S(2)}, u32[]{:S(2)}) collective-permute-start(bf16[2,192,384]{2,1,0:T(8,128)(2,1)} %dynamic-slice_bitcast_fusion.11), channel_id=1, source_target_pairs={{0,2},{1,3},{2,0},{3,1},{4,6},{5,7},{6,4},{7,5},{8,10},{9,11},{10,... | collective-permute-start | bytes 884744 | tf_op jit(solution)/shard_map/ppermute | solution.py:89
  418.3 43.4 %collective-permute-start.33 = (bf16[2,2,2,88,768]{4,3,2,1,0:T(8,128)(2,1)}, bf16[2,2,2,88,768]{4,3,2,1,0:T(8,128)(2,1)}, u32[]{:S(2)}, u32[]{:S(2)}) collective-permute-start(bf16[2,2,2,88,768]{4,3,2,1,0:T(8,128)(2,1)} %dynamic-slice_bitcast_fusion.2), channel_id=1, source_target_pairs={{0,1},{1,0},{2,3},{3,2},{4,5},{5,4},{6,7},{7,6},{8,9},{9,8},{10,11... | collective-permute-start | bytes 3244040 | tf_op jit(solution)/shard_map/ppermute | solution.py:89
  439.5 22.2 %collective-permute-start.32 = (bf16[2,48,1792]{2,1,0:T(8,128)(2,1)}, bf16[2,48,1792]{2,1,0:T(8,128)(2,1)}, u32[]{:S(2)}, u32[]{:S(2)}) collective-permute-start(bf16[2,48,1792]{2,1,0:T(8,128)(2,1)} %dynamic-slice_bitcast_fusion.10), channel_id=1, source_target_pairs={{0,2},{1,3},{2,0},{3,1},{4,6},{5,7},{6,4},{7,5},{8,10},{9,11},{10,... | collective-permute-start | bytes 1032200 | tf_op jit(solution)/shard_map/ppermute | solution.py:89
  441.4 51.6 %collective-permute-start.48 = (bf16[2,2,2,48,1152]{4,3,2,1,0:T(8,128)(2,1)}, bf16[2,2,2,48,1152]{4,3,2,1,0:T(8,128)(2,1)}, u32[]{:S(2)}, u32[]{:S(2)}) collective-permute-start(bf16[2,2,2,48,1152]{4,3,2,1,0:T(8,128)(2,1)} %dynamic-slice_bitcast_fusion.3), channel_id=1, source_target_pairs={{0,16},{8,24},{16,0},{24,8},{1,17},{9,25},{17,1},{25,9},{2,18},{10... | collective-permute-start | bytes 2654216 | tf_op jit(solution)/shard_map/ppermute | solution.py:89
  470.4 25.3 %collective-permute-start.59 = (bf16[2,2,88,768]{3,2,1,0:T(8,128)(2,1)S(1)}, bf16[2,2,88,768]{3,2,1,0:T(8,128)(2,1)S(1)}, u32[]{:S(2)}, u32[]{:S(2)}) collective-permute-start(bf16[2,2,88,768]{3,2,1,0:T(8,128)(2,1)S(1)} %dynamic-slice_bitcast_fusion.6), channel_id=1, source_target_pairs={{0,16},{8,24},{16,0},{24,8},{1,17},{9,25},{17,1},{25,9},{2,18},{10... | collective-permute-start | bytes 1622024 | tf_op jit(solution)/shard_map/ppermute | solution.py:89
  472.8 34.4 %collective-permute-start.34 = (bf16[768,512]{0,1:T(8,128)(2,1)}, bf16[768,512]{0,1:T(8,128)(2,1)}, u32[]{:S(2)}, u32[]{:S(2)}) collective-permute-start(bf16[768,512]{0,1:T(8,128)(2,1)} %fusion.46), channel_id=1, source_target_pairs={{0,8},{8,0},{16,24},{24,16},{1,9},{9,1},{17,25},{25,17},{2,10},{10... | collective-permute-start | bytes 2359304 | tf_op jit(solution)/shard_map/ppermute | solution.py:89
  479.5 38.2 %collective-permute-start.41 = (bf16[768,640]{0,1:T(8,128)(2,1)}, bf16[768,640]{0,1:T(8,128)(2,1)}, u32[]{:S(2)}, u32[]{:S(2)}) collective-permute-start(bf16[768,640]{0,1:T(8,128)(2,1)} %fusion.45), channel_id=1, source_target_pairs={{0,8},{8,0},{16,24},{24,16},{1,9},{9,1},{17,25},{25,17},{2,10},{10... | collective-permute-start | bytes 2949128 | tf_op jit(solution)/shard_map/ppermute | solution.py:89
  495.8 20.1 %collective-permute-start.49 = (bf16[2,2,48,1152]{3,2,1,0:T(8,128)(2,1)}, bf16[2,2,48,1152]{3,2,1,0:T(8,128)(2,1)}, u32[]{:S(2)}, u32[]{:S(2)}) collective-permute-start(bf16[2,2,48,1152]{3,2,1,0:T(8,128)(2,1)} %dynamic-slice_bitcast_fusion.8), channel_id=1, source_target_pairs={{0,1},{1,0},{2,3},{3,2},{4,5},{5,4},{6,7},{7,6},{8,9},{9,8},{10,11... | collective-permute-start | bytes 1327112 | tf_op jit(solution)/shard_map/ppermute | solution.py:89
  522.2 23.9 %collective-permute-start.42 = (bf16[2,2,2,48,640]{4,3,2,1,0:T(8,128)(2,1)S(1)}, bf16[2,2,2,48,640]{4,3,2,1,0:T(8,128)(2,1)S(1)}, u32[]{:S(2)}, u32[]{:S(2)}) collective-permute-start(bf16[2,2,2,48,640]{4,3,2,1,0:T(8,128)(2,1)S(1)} %dynamic-slice_bitcast_fusion.7), channel_id=1, source_target_pairs={{0,1},{1,0},{2,3},{3,2},{4,5},{5,4},{6,7},{7,6},{8,9},{9,8},{10,11... | collective-permute-start | bytes 1474568 | tf_op jit(solution)/shard_map/ppermute | solution.py:89
  (193 other events, 1546.0 us)
Sparse Core Ops, SparseCore 0:
  11.7 87.9 all-gather.2
  103.1 73.8 all-gather.4

commit v3 on v2

--- a/solution.py
+++ b/solution.py
@@ -99,59 +99,102 @@
     return [1 << k for k in range(count.bit_length() - 1)]
 
 
-def route(first):
-    rep = [("rep", step) for step in bits("rep")[1:]]
-    fsdp = [("fsdp", step) for step in bits("fsdp")]
-    return rep + fsdp if first == "rep" else fsdp[:1] + rep + fsdp[1:]
-
-
 def add(left, right):
     return (left.astype(jnp.float32) + right.astype(jnp.float32)).astype(jnp.bfloat16)
 
 
-class Flow:
-    def __init__(self, sent, kept, first):
-        self.kept = kept
-        self.got = swap(sent, "rep", 1)
-        self.left = route(first)
-        fsdp = [("fsdp", step) for step in reversed(bits("fsdp"))]
-        rep = [("rep", step) for step in reversed(bits("rep")[1:])]
-        self.places = fsdp + rep
-        rows = kept.shape[0] // 2 ** len(self.places)
-        self.shape = (2,) * len(self.places) + (rows, kept.shape[1])
-
-    def advance(self):
-        if self.got is None:
-            return
-        total = add(self.kept, self.got)
-        if self.shape is not None:
-            total = total.reshape(self.shape)
-            self.shape = None
-        self.kept, self.got = total, None
-        if self.left:
-            (axis, step), self.left = self.left[0], self.left[1:]
-            at = self.places.index((axis, step))
-            self.places = self.places[:at] + self.places[at + 1 :]
-            here = bit_of(axis, step)
-            away = lax.dynamic_index_in_dim(total, 1 - here, at, False)
-            self.kept = lax.dynamic_index_in_dim(total, here, at, False)
-            self.got = swap(away, axis, step)
-
-    def shard(self):
-        whole = self.kept
-        for step in bits("rep")[1:]:
-            whole = join(whole, 0, "rep", step)
-        whole = whole.reshape(-1, whole.shape[-1])
-        return join(whole, 1, "rep", 1).reshape(whole.shape[0], -1).astype(jnp.float32)
-
-
-def tie(value, *flows):
-    flows = [flow for flow in flows if flow.got is not None]
-    tied = lax.optimization_barrier((value, *[flow.got for flow in flows]))
-    for flow, got in zip(flows, tied[1:]):
-        flow.got = got
-        flow.advance()
+class Task:
+    def __init__(self, steps):
+        self.steps = steps
+        self.result = None
+        self.got = next(steps)
+
+    def advance(self, got):
+        try:
+            self.got = self.steps.send(got)
+        except StopIteration as end:
+            self.got, self.result = None, end.value
+
+
+def tie(value, *tasks):
+    tasks = [task for task in tasks if task.got is not None]
+    tied = lax.optimization_barrier((value, *[task.got for task in tasks]))
+    for task, got in zip(tasks, tied[1:]):
+        task.advance(got)
     return tied[0]
+
+
+def lockstep(*tasks):
+    tasks = [task for task in tasks if task.got is not None]
+    tied = lax.optimization_barrier(tuple(task.got for task in tasks))
+    for task, got in zip(tasks, tied):
+        task.advance(got)
+
+
+def flow(sent, kept, first):
+    got = yield swap(sent, "rep", 1)
+    total = add(kept, got)
+    fsdp = [("fsdp", step) for step in reversed(bits("fsdp"))]
+    rep = [("rep", step) for step in reversed(bits("rep")[1:])]
+    places = fsdp + rep
+    rows = total.shape[0] // 2 ** len(places)
+    total = total.reshape((2,) * len(places) + (rows, total.shape[1]))
+    for axis, step in rep + fsdp[-1:] if first == "rep" else fsdp[-1:] + rep:
+        total, away = parted(total, places.index((axis, step)), axis, step)
+        places.remove((axis, step))
+        got = yield swap(away, axis, step)
+        total = add(total, got)
+    return total
+
+
+def parted(total, at, axis, step):
+    here = bit_of(axis, step)
+    away = lax.dynamic_index_in_dim(total, 1 - here, at, False)
+    return lax.dynamic_index_in_dim(total, here, at, False), away
+
+
+def shards(blocks, rows):
+    total = jnp.concatenate([laid_out(block, rows) for block in blocks], axis=-1)
+    left = list(reversed(bits("fsdp")[1:]))
+    for step in bits("fsdp")[1:]:
+        total, away = parted(total, left.index(step), "fsdp", step)
+        left.remove(step)
+        got = yield swap(away, "fsdp", step)
+        total = add(total, got)
+    total = total[None]
+    for step in bits("rep")[1:]:
+        total = yield from joined(total, 0, "rep", step)
+        total = total.reshape(-1, *total.shape[2:])
+    total = yield from joined(total, 2, "rep", 1)
+    chips = total.shape[0]
+    results = []
+    start = 0
+    for block in blocks:
+        height, columns = block.shape[-2:]
+        count = -(-height // rows)
+        part = total[..., start : start + count * columns].astype(jnp.float32)
+        start += count * columns
+        part = part.reshape(chips, rows, 2, count, columns).transpose(0, 3, 1, 2, 4)
+        part = part.reshape(chips, count * rows, 2 * columns)[:, :height]
+        results.append(part.reshape(chips * height, 2 * columns))
+    return results
+
+
+def laid_out(block, rows):
+    height, columns = block.shape[-2:]
+    count = -(-height // rows)
+    if count == 1:
+        return block
+    lead = block.shape[:-2]
+    block = jnp.pad(block, [(0, 0)] * len(lead) + [(0, count * rows - height), (0, 0)])
+    block = block.reshape(*lead, count, rows, columns)
+    return jnp.moveaxis(block, -3, -2).reshape(*lead, rows, count * columns)
+
+
+def joined(values, at, axis, step):
+    theirs = yield swap(values, axis, step)
+    first = bit_of(axis, step) == 0
+    return jnp.stack([jnp.where(first, values, theirs), jnp.where(first, theirs, values)], axis=at)
 
 
 def gradient_halves(values, gradient):
@@ -204,13 +247,6 @@
     return values
 
 
-def sum_everywhere(values):
-    for axis in ("rep", "fsdp"):
-        for step in bits(axis):
-            values = values + swap(values, axis, step)
-    return values
-
-
 def gather_rows(shard):
     part = shard.shape[0] // lax.axis_size("rep")
     mine = lax.dynamic_slice_in_dim(shard, lax.axis_index("rep") * part, part, 0)
@@ -222,46 +258,42 @@
     return lax.dynamic_slice_in_dim(shard, at * size, size, axis)
 
 
-def exchange_rows(shard, first):
-    count = lax.axis_size("rep")
-    mine = part_of(shard, count, lax.axis_index("rep"), 0)
+def fetch_fsdp(mine, first):
     rows, columns = mine.shape
     whole = mine[None]
-    fsdp, rep = bits("fsdp"), bits("rep")
-    for step in fsdp[1:]:
-        whole = join(whole, 0, "fsdp", step).reshape(-1, rows, columns)
-    if first == "rep":
-        whole = whole[:, None]
-        for step in rep[1:]:
-            whole = join(whole, 1, "rep", step).reshape(whole.shape[0], -1, rows, columns)
-        whole = join(whole, 1, "fsdp", 1)
-    else:
-        whole = join(whole, 1, "fsdp", 1)[:, :, None]
-        for step in rep[1:]:
-            whole = join(whole, 2, "rep", step).reshape(*whole.shape[:2], -1, rows, columns)
-    whole = join(whole, 3, "rep", 1)
-    return whole.reshape(-1, columns)
+    for step in reversed(bits("fsdp")[1:]):
+        whole = yield from joined(whole, 1, "fsdp", step)
+        whole = whole.reshape(-1, rows, columns)
+    low, rep = bits("fsdp")[:1], bits("rep")[1:]
+    whole = whole[:, None, None]
+    for axis, step in (
+        [("rep", step) for step in rep] + [("fsdp", step) for step in low]
+        if first == "rep"
+        else [("fsdp", step) for step in low] + [("rep", step) for step in rep]
+    ):
+        whole = yield from joined(whole, 1 if axis == "fsdp" else 2, axis, step)
+        shape = whole.shape
+        whole = (
+            whole.reshape(shape[0], -1, *shape[3:])
+            if axis == "fsdp"
+            else whole.reshape(*shape[:2], -1, *shape[4:])
+        )
+    return whole.reshape(-1, whole.shape[2], rows, columns)
+
+
+def exchange_rows(shard, first):
+    mine = part_of(shard, lax.axis_size("rep"), lax.axis_index("rep"), 0)
+    whole = yield from fetch_fsdp(mine, first)
+    whole = yield from joined(whole, 2, "rep", 1)
+    return whole.reshape(-1, shard.shape[1])
 
 
 def exchange_columns(shard, first):
-    fsdp, rep = bits("fsdp"), bits("rep")
     mine = part_of(shard, 2, bit_of("rep", 1), 1)
-    mine = part_of(mine, 2 ** len(rep[1:]), lax.axis_index("rep") // 2, 0)
-    rows, columns = mine.shape
-    whole = mine[None]
-    for step in fsdp[1:]:
-        whole = join(whole, 0, "fsdp", step).reshape(-1, rows, columns)
-    if first == "rep":
-        whole = whole[:, None]
-        for step in rep[1:]:
-            whole = join(whole, 1, "rep", step).reshape(whole.shape[0], -1, rows, columns)
-        whole = join(whole, 1, "fsdp", 1)
-    else:
-        whole = join(whole, 1, "fsdp", 1)[:, :, None]
-        for step in rep[1:]:
-            whole = join(whole, 2, "rep", step).reshape(*whole.shape[:2], -1, rows, columns)
-    whole = whole.reshape(-1, columns)
-    theirs = swap(whole, "rep", 1)
+    mine = part_of(mine, lax.axis_size("rep") // 2, lax.axis_index("rep") // 2, 0)
+    whole = yield from fetch_fsdp(mine, first)
+    whole = whole.reshape(-1, mine.shape[1])
+    theirs = yield swap(whole, "rep", 1)
     core = bit_of("rep", 1) == 0
     return (jnp.where(core, whole, theirs), jnp.where(core, theirs, whole))
 
@@ -405,7 +437,6 @@
     emb = picture_mapping_matrix.shape[1]
     w_self = gather_rows(jnp.concatenate([attend_triple_matrix, inward_result_matrix], axis=1))
     w_qkv, w_self_out = w_self[:, : 3 * width], w_self[:, 3 * width :]
-    w_keys, w_values = exchange_columns(visual_lookup_pairs, "rep")
     w_rest = gather_rows(
         jnp.concatenate(
             [
@@ -421,7 +452,13 @@
     w_asker, w_cross_out = w_rest[:, :width], w_rest[:, width : 2 * width]
     w_up = w_rest[:, 2 * width : -2 * emb]
     w_image, w_text = w_rest[:, -2 * emb : -emb], w_rest[:, -emb:]
-    w_down = exchange_rows(narrowing_matrix, "fsdp")
+    pairs = Task(exchange_columns(visual_lookup_pairs, "rep"))
+    narrow = Task(exchange_rows(narrowing_matrix, "fsdp"))
+    for task in (pairs, narrow):
+        while task.got is not None:
+            task.advance(task.got)
+    w_keys, w_values = pairs.result
+    w_down = narrow.result
 
     qkv = project(sequence_entries, w_qkv).astype(bf16)
     q_self, k_self, v_self = (qkv[..., i * width : (i + 1) * width] for i in range(3))
@@ -511,7 +548,7 @@
         third_sum, feed_scale, feed_shift, grad_final
     )
     grad_third = grad_third_sum.astype(bf16)
-    down = Flow(*gradient_halves(activated, grad_third), "fsdp")
+    down = Task(flow(*gradient_halves(activated, grad_third), "fsdp"))
     grad_active = project_back(grad_third, w_down)
     _, gelu_pull = jax.vjp(exact_gelu, pre_act)
     grad_pre = gelu_pull(grad_active)[0].astype(bf16)
@@ -520,7 +557,7 @@
         [outer_sum(pooled_low, grad_image_raw), outer_sum(caption_low, grad_text_raw)], axis=1
     ).astype(bf16)
     ends_halves = (part_of(ends, 2, 1 - bit_of("rep", 1), 1), part_of(ends, 2, bit_of("rep", 1), 1))
-    up = Flow(*side_by_side(gradient_halves(merged_low, grad_pre), ends_halves), "rep")
+    up = Task(flow(*side_by_side(gradient_halves(merged_low, grad_pre), ends_halves), "rep"))
     grad_merged = grad_third_sum + project_back(grad_pre, w_up)
     grad_merged = tie(grad_merged, up)
 
@@ -538,38 +575,30 @@
     core_zero = bit_of("rep", 1) == 0
     grad_key = grad_key.astype(bf16)
     grad_value = grad_value.astype(bf16)
-    keyval = Flow(
+    keyval = Task(flow(
         outer_sum(picture_descriptors, jnp.where(core_zero, grad_value, grad_key)).astype(bf16),
         outer_sum(picture_descriptors, jnp.where(core_zero, grad_key, grad_value)).astype(bf16),
         "fsdp",
-    )
+    ))
     asker_halves = gradient_halves(head_low, grad_asked)
     grad_head = grad_second_sum + project_back(grad_asked, w_asker)
     grad_inner = jnp.concatenate([grad_head, grad_merged[:, QUERY:]], axis=1)
-    grad_inner = tie(grad_inner, down, keyval)
+    grad_inner = tie(grad_inner, keyval)
 
     grad_first_sum, self_gain, self_shift_grad = norm_back(
         first_sum, self_scale, self_shift, grad_inner
     )
     grad_first = grad_first_sum.astype(bf16)
-    middle = Flow(
+    middle = Task(flow(
         *side_by_side(cross_out_halves, asker_halves, gradient_halves(self_mix, grad_first)), "rep"
-    )
+    ))
     grad_self_mix = project_back(grad_first, w_self_out).astype(bf16)
-    grad_self_mix = tie(grad_self_mix, up, middle)
+    grad_self_mix = tie(grad_self_mix, down, up, middle)
     grad_q, grad_k, grad_v = attend_back(q_self, k_self, v_self, self_probs, grad_self_mix)
+    grad_q = tie(grad_q, keyval)
+    grad_v = tie(grad_v, middle)
     grad_qkv = jnp.concatenate([grad_q, grad_k, grad_v], axis=-1).astype(bf16)
-    grad_qkv = tie(grad_qkv, down, up, keyval)
-    cut = 4 * grad_qkv.shape[-1] // 9
-    left = Flow(*gradient_halves(sequence_entries, grad_qkv[..., :cut]), "rep")
-    right = Flow(*gradient_halves(sequence_entries, grad_qkv[..., cut:]), "fsdp")
-    flows = (down, up, keyval, middle, left, right)
-    incoming = grad_first_sum + project_back(grad_qkv, w_qkv)
-    while any(flow.got is not None for flow in flows):
-        for flow in flows:
-            flow.advance()
-
-    early = (
+    vector_grads = (
         column_sum(grad_pre),
         column_sum(grad_third),
         feed_gain,
@@ -579,18 +608,50 @@
         cross_shift_grad,
         column_sum(grad_image_raw),
         column_sum(grad_text_raw),
-    )
-    late = (column_sum(grad_first), self_gain, self_shift_grad)
-    shards = []
-    for group in (early, late):
-        summed = sum_everywhere(jnp.concatenate(group)[None])[0]
-        offset = 0
-        for vector in group:
-            size = vector.shape[0]
-            share = size // lax.axis_size("fsdp")
-            start = offset + lax.axis_index("fsdp") * share
-            shards.append(lax.dynamic_slice_in_dim(summed, start, share, 0))
-            offset += size
+        column_sum(grad_first),
+        self_gain,
+        self_shift_grad,
+    )
+    fsdp = lax.axis_size("fsdp")
+    chips = lax.axis_size("rep") // 2
+    share = width // fsdp
+    packed = jnp.concatenate([vector.reshape(fsdp, -1) for vector in vector_grads], axis=1)
+    lanes = 128
+    slots = -(-packed.shape[1] // (2 * chips * lanes))
+    assert slots <= share // chips
+    packed = jnp.pad(packed, [(0, 0), (0, 2 * chips * slots * lanes - packed.shape[1])])
+    packed = packed.astype(bf16).reshape(fsdp, 2, chips, slots, lanes)
+    packed = jnp.pad(packed, [(0, 0)] * 3 + [(0, share // chips - slots), (0, 0)])
+    packed = jnp.moveaxis(packed, 1, 0).reshape(2, width, lanes)
+    core = bit_of("rep", 1)
+    packed_halves = tuple(
+        lax.dynamic_index_in_dim(packed, at, 0, False) for at in (1 - core, core)
+    )
+    last = Task(
+        flow(*side_by_side(gradient_halves(sequence_entries, grad_qkv), packed_halves), "fsdp")
+    )
+    incoming = grad_first_sum + project_back(grad_qkv, w_qkv)
+    rows_here = share // chips
+    lockstep(last, keyval, middle)
+    early = Task(shards((up.result, down.result, keyval.result), rows_here))
+    while last.got is not None:
+        lockstep(last, early)
+    late = Task(shards((middle.result, last.result), rows_here))
+    while late.got is not None or early.got is not None:
+        lockstep(late, early)
+    up_shard, down_shard, keyval_shard = early.result
+    middle_shard, last_shard = late.result
+    up_grad, ends_grad = blocks_of(up_shard, (widening_matrix.shape[1], 2 * emb))
+    cross_out_grad, asker_grad, self_out_grad = blocks_of(middle_shard, (width,) * 3)
+    qkv_grad, packed = blocks_of(last_shard, (3 * width, 2 * lanes))
+    packed = packed.reshape(chips, rows_here, 2, lanes)[:, :slots]
+    packed = jnp.moveaxis(packed, 2, 0).reshape(-1)
+    vector_shards = []
+    offset = 0
+    for vector in vector_grads:
+        size = vector.shape[0] // fsdp
+        vector_shards.append(packed[offset : offset + size])
+        offset += size
     (
         up_bias,
         down_bias,
@@ -604,12 +665,7 @@
         self_bias,
         self_gain,
         self_shift_grad,
-    ) = shards
-    up_shard, middle_shard = up.shard(), middle.shard()
-    inner_width = up_bias.shape[0] * lax.axis_size("fsdp")
-    up_grad, ends_grad = blocks_of(up_shard, (inner_width, 2 * emb))
-    cross_out_grad, asker_grad, self_out_grad = blocks_of(middle_shard, (width,) * 3)
-    qkv_grad = jnp.concatenate([left.shard(), right.shard()], axis=1)
+    ) = vector_shards
     return (
         out,
         incoming,
@@ -619,14 +675,14 @@
         self_gain,
         self_shift_grad,
         asker_grad,
-        keyval.shard(),
+        keyval_shard,
         cross_out_grad,
         cross_bias,
         cross_gain,
         cross_shift_grad,
         up_grad,
         up_bias,
-        down.shard(),
+        down_shard,
         down_bias,
         feed_gain,
         feed_shift_grad,

time: 592 us -> 585 us (0.988)
  starting transfers between devices: 71.7 us -> 45.9 us
  local copies, waits for them, and re-layouts: 85.6 us -> 105 us
    ppermute x75 -> x46, starting transfers between devices: 71.6 us -> 45.8 us  [swap(): return lax.ppermute(values, axis, [(i, i ^ step) for i in range(count)])]
    another operation x0 -> x8, local copies, waits for them, and re-layouts: none -> 10.9 us  [the longest x5 6.08 us: shards(): results.append(part.reshape(chips * height, 2 * columns))]
    another operation x54 -> x23, other arithmetic: 14.9 us -> 5.13 us  [join(): jnp.stack([jnp.where(first, values, theirs), jnp.where(first, theirs, val...]
    another operation x0 -> x21, other arithmetic: none -> 7.71 us  [the longest x17 7.34 us: joined(): jnp.stack([jnp.where(first, values, theirs), jnp.where(first, theirs, val...]
    dot_general x20 -> x18, matrix products: 38.5 us -> 32.5 us  [outer_sum(): lax.dot_general(flat_values, flat_gradient, (((0,), (0,)), ((), ())), pre...]
    unnamed x291 -> x289, local copies, waits for them, and re-layouts: 12.8 us -> 18.5 us
    ppermute x75 -> x46, waiting for transfers between devices: 161 us -> 165 us  [swap(): return lax.ppermute(values, axis, [(i, i ^ step) for i in range(count)])]
    convert_element_type x28 -> x17, other arithmetic: 23.3 us -> 26.4 us  [add(): (left.astype(jnp.float32) + right.astype(jnp.float32)).astype(jnp.bfloat16)]
  transfers between devices with their start and end apart: 77 -> 48, of which waited for: 35 -> 23; matrix products, arithmetic and copies ran while one was open for 46% -> 45% of each run, Pallas kernels for 0% -> 0%
where the time goes in v3:
time: 585 us; the launch traced here: 576 us
  waiting for transfers between devices  180 us (31%)
  matrix products  129 us (22%)
  local copies, waits for them, and re-layouts  105 us (18%)
  other arithmetic  95.8 us (16%)
  starting transfers between devices  45.9 us (8%)
  between operations  21.2 us (4%)
    ppermute x46, waiting for transfers between devices, swap(): return lax.ppermute(values, axis, [(i, i ^ step) for i in range(count)])  165 us
    ppermute x46, starting transfers between devices, swap(): return lax.ppermute(values, axis, [(i, i ^ step) for i in range(count)])  45.8 us
    dot_general x10, matrix products, project(): jnp.einsum('...d,df->...f', values, matrix, preferred_element_type=jnp.fl...  36.5 us
    dot_general x18, matrix products, outer_sum(): lax.dot_general(flat_values, flat_gradient, (((0,), (0,)), ((), ())), pre...  32.5 us
    dot_general x8, matrix products, project_back(): jnp.einsum('...f,df->...d', gradient, matrix, preferred_element_type=jnp....  27.5 us
    convert_element_type x17, other arithmetic, add(): (left.astype(jnp.float32) + right.astype(jnp.float32)).astype(jnp.bfloat16)  26.4 us
    unnamed x289, local copies, waits for them, and re-layouts  18.5 us
    all_gather x2, waiting for transfers between devices, gather_rows(): return lax.all_gather(mine, ('fsdp', 'rep'), axis=0, tiled=True)  14.8 us
  transfers between devices with their start and end apart: 48, of which 23 were waited for; matrix products, arithmetic and copies ran while one was open for 45% of the time, Pallas kernels for 0%

profile of v3, /device:TPU:0, one launch (start us, length us, event | category | flops | bytes accessed | tf_op | source)
XLA Modules:
  0.0 576.2 jit_solution(13871624757262043976)
XLA Ops:
  24.7 6.9 %collective-permute-done.3 = bf16[1,88,768]{2,1,0:T(8,128)(2,1)S(1)} collective-permute-done((bf16[1,88,768]{2,1,0:T(8,128)(2,1)S(1)}, bf16[1,88,768]{2,1,0:T(8,128)(2,1)S(1)}, u32[]{:S(2)}, u32[]{:S(2)}) %collective-permute-start.3) | collective-permute-done | bytes 135200 | tf_op jit(solution)/shard_map/ppermute | solution.py:89
  35.8 5.4 collective-permute-done.4
  43.5 5.9 %collective-permute-done.9 = bf16[2,96,768]{2,1,0:T(8,128)(2,1)S(1)} collective-permute-done((bf16[2,96,768]{2,1,0:T(8,128)(2,1)S(1)}, bf16[2,96,768]{2,1,0:T(8,128)(2,1)S(1)}, u32[]{:S(2)}, u32[]{:S(2)}) %collective-permute-start.9) | collective-permute-done | bytes 294944 | tf_op jit(solution)/shard_map/ppermute | solution.py:89
  51.2 7.9 %collective-permute-done.5 = bf16[4,1,1,88,768]{4,3,0,2,1:T(8,128)(2,1)S(1)} collective-permute-done((bf16[4,1,1,88,768]{4,3,0,2,1:T(8,128)(2,1)S(1)}, bf16[4,1,1,88,768]{4,3,0,2,1:T(8,128)(2,1)S(1)}, u32[]{:S(2)}, u32[]{:S(2)}) %collective-permute-start.5) | collective-permute-done | bytes 540704 | tf_op jit(solution)/shard_map/ppermute | solution.py:89
  67.6 28.5 %collective-permute-done.6 = bf16[4,1,2,88,768]{4,3,0,2,1:T(8,128)(2,1)S(1)} collective-permute-done((bf16[4,1,2,88,768]{4,3,0,2,1:T(8,128)(2,1)S(1)}, bf16[4,1,2,88,768]{4,3,0,2,1:T(8,128)(2,1)S(1)}, u32[]{:S(2)}, u32[]{:S(2)}) %collective-permute-start.6) | collective-permute-done | bytes 1081376 | tf_op jit(solution)/shard_map/ppermute | solution.py:89
  108.8 7.4 %convert_bitcast_fusion.1 = bf16[5,257,768]{2,1,0:T(8,128)(2,1)} fusion(bf16[5,257,1408]{2,1,0:T(8,128)(2,1)} %param.28, bf16[1408,768]{1,0:T(8,128)(2,1)} %collective-permute-done.7, bf16[1408,768]{1,0:T(8,128)(2,1)} %bitcast.28, pred[]{:T(512)S(6)} %eq.159), kind=kOutput, calls=%fused_computation.90 | convolution fusion | flops 2781122304 | bytes 9917697 | tf_op jit(solution)/shard_map/...d,df->...f/dot_general | solution.py:15
  120.9 7.4 %convert_bitcast_fusion = bf16[5,257,768]{2,1,0:T(8,128)(2,1)} fusion(bf16[5,257,1408]{2,1,0:T(8,128)(2,1)} %param.28, bf16[1408,768]{1,0:T(8,128)(2,1)} %bitcast.28, bf16[1408,768]{1,0:T(8,128)(2,1)} %collective-permute-done.7, pred[]{:T(512)S(6)} %eq.159), kind=kOutput, calls=%fused_computation.89 | convolution fusion | flops 2781122304 | bytes 9917697 | tf_op jit(solution)/shard_map/...d,df->...f/dot_general | solution.py:15
  154.8 14.8 %all-gather.5.cloned.1.call-done = bf16[768,5120]{1,0:T(8,128)(2,1)} async-done(((bf16[24,5120]{1,0:T(8,128)(2,1)}), bf16[768,5120]{1,0:T(8,128)(2,1)}) %all-gather.5.cloned.1.call-update) | async-done | bytes 7864336 | tf_op jit(solution)/shard_map/all_gather | solution.py:253
  175.2 10.5 %fusion.175 = (f32[5,12,32]{2,1,0:T(8,128)S(1)}, f32[5,12,32,257]{3,2,1,0:T(8,128)S(1)}) fusion(f32[5,12,32,257]{3,2,1,0:T(8,128)S(1)} %fusion.95), kind=kOutput, calls=%fused_computation.469 | output fusion | flops 1974016 | bytes 3955200 | tf_op jit(solution)/shard_map/sub | solution.py:304
  193.1 6.5 %fusion.50 = (u8[96,3072]{1,0:T(8,128)(4,1)S(1)}, u8[96,3072]{1,0:T(8,128)(4,1)S(1)}, f32[5,96,3072]{2,1,0:T(8,128)S(1)}) fusion(f32[3072]{0:T(1024)S(1)} %reshape.679, bf16[5,96,768]{2,1,0:T(8,128)(2,1)S(1)} %fusion.59, bf16[768,5120]{1,0:T(8,128)(2,1)} %all-gather.5.cloned.1.call-done), kind=kOutput, calls=%fused_computation.125 | convolution fusion | flops 2284978176 | bytes 11956224 | tf_op jit(solution)/shard_map/...d,df->...f/dot_general | solution.py:15
  199.6 14.6 %multiply_convert_fusion.1 = (bf16[5,96,3072]{2,1,0:T(8,128)(2,1)S(1)}, f32[5,96,3072]{2,1,0:T(8,128)}) fusion(f32[5,96,3072]{2,1,0:T(8,128)S(1)} %get-tuple-element.223, f32[3072]{0:T(1024)S(1)} %reshape.679, u8[96,3072]{1,0:T(8,128)(4,1)S(1)} %get-tuple-element.81, u8[96,3072]{1,0:T(8,128)(4,1)S(1)} %get-tuple-element.80), kind=kLoop, calls=%fused_computation.11 | loop fusion | flops 104693760 | bytes 15347712 | tf_op jit(solution)/shard_map/convert_element_type | solution.py:481
  272.6 8.4 %add_convert_fusion = bf16[5,96,3072]{2,1,0:T(8,128)(2,1)S(1)} fusion(f32[5,96,3072]{2,1,0:T(8,128)} %get-tuple-element.112, f32[5,96,3072]{2,1,0:T(8,128)} %copy-done.16, bf16[5,96,768]{2,1,0:T(8,128)(2,1)S(1)} %get-tuple-element.102, bf16[3072,768,1]{1,0,2:T(8,128)(2,1)} %bitcast.508, f32[3072]{0:T(1024)S(1)} %copy-done.98), kind=kOutput, calls=%fused_computation.10 | convolution fusion | flops 2287042560 | bytes 20213760 | tf_op jit(solution)/shard_map/...f,df->...d/dot_general | solution.py:19
  293.7 5.1 convolution_convert_fusion.1
  311.0 4.9 add_add_fusion.4
  331.1 5.1 fusion.14
  341.0 5.3 bitcast_convert_fusion
  351.5 20.8 %collective-permute-done.26 = bf16[2,2,2,48,1792]{4,3,2,1,0:T(8,128)(2,1)} collective-permute-done((bf16[2,2,2,48,1792]{4,3,2,1,0:T(8,128)(2,1)}, bf16[2,2,2,48,1792]{4,3,2,1,0:T(8,128)(2,1)}, u32[]{:S(2)}, u32[]{:S(2)}) %collective-permute-start.26) | collective-permute-done | bytes 1376288 | tf_op jit(solution)/shard_map/ppermute | solution.py:89
  415.4 9.5 %collective-permute-done.31 = bf16[2,2,2,88,768]{4,3,2,1,0:T(8,128)(2,1)} collective-permute-done((bf16[2,2,2,88,768]{4,3,2,1,0:T(8,128)(2,1)}, bf16[2,2,2,88,768]{4,3,2,1,0:T(8,128)(2,1)}, u32[]{:S(2)}, u32[]{:S(2)}) %collective-permute-start.31) | collective-permute-done | bytes 1081376 | tf_op jit(solution)/shard_map/ppermute | solution.py:89
  452.8 5.9 %collective-permute-done.34 = bf16[2,2,88,768]{3,2,1,0:T(8,128)(2,1)S(1)} collective-permute-done((bf16[2,2,88,768]{3,2,1,0:T(8,128)(2,1)S(1)}, bf16[2,2,88,768]{3,2,1,0:T(8,128)(2,1)S(1)}, u32[]{:S(2)}, u32[]{:S(2)}) %collective-permute-start.34) | collective-permute-done | bytes 540704 | tf_op jit(solution)/shard_map/ppermute | solution.py:89
  473.5 19.8 %collective-permute-done.37 = bf16[2,48,4864]{2,1,0:T(8,128)(2,1)} collective-permute-done((bf16[2,48,4864]{2,1,0:T(8,128)(2,1)}, bf16[2,48,4864]{2,1,0:T(8,128)(2,1)}, u32[]{:S(2)}, u32[]{:S(2)}) %collective-permute-start.37) | collective-permute-done | bytes 933920 | tf_op jit(solution)/shard_map/ppermute | solution.py:89
  499.6 18.9 %collective-permute-done.39 = bf16[48,4864]{1,0:T(8,128)(2,1)S(1)} collective-permute-done((bf16[48,4864]{1,0:T(8,128)(2,1)S(1)}, bf16[48,4864]{1,0:T(8,128)(2,1)S(1)}, u32[]{:S(2)}, u32[]{:S(2)}) %collective-permute-start.39) | collective-permute-done | bytes 466976 | tf_op jit(solution)/shard_map/ppermute | solution.py:89
  523.8 7.7 %collective-permute-done.40 = bf16[2,48,2432]{2,1,0:T(8,128)(2,1)} collective-permute-done((bf16[2,48,2432]{2,1,0:T(8,128)(2,1)}, bf16[2,48,2432]{2,1,0:T(8,128)(2,1)}, u32[]{:S(2)}, u32[]{:S(2)}) %collective-permute-start.40) | collective-permute-done | bytes 466976 | tf_op jit(solution)/shard_map/ppermute | solution.py:89
  536.4 5.0 fusion.51
  541.4 6.7 %collective-permute-done.42 = bf16[48,2432]{1,0:T(8,128)(2,1)S(1)} collective-permute-done((bf16[48,2432]{1,0:T(8,128)(2,1)S(1)}, bf16[48,2432]{1,0:T(8,128)(2,1)S(1)}, u32[]{:S(2)}, u32[]{:S(2)}) %collective-permute-start.42) | collective-permute-done | bytes 233504 | tf_op jit(solution)/shard_map/ppermute | solution.py:89
  (686 shorter events, 315.8 us)
Async XLA Ops:
  7.4 130.4 %all-gather.3.cloned.1.call-start = ((), (), s32[]{:S(2)}) async-start(), calls=%async_computation | async-start | bytes 4866048 | tf_op jit(solution)/shard_map/all_gather | solution.py:253
  9.2 160.4 %all-gather.5.cloned.1.call-start = ((), (), s32[]{:S(2)}) async-start(), calls=%async_computation.1 | async-start | bytes 8110080 | tf_op jit(solution)/shard_map/all_gather | solution.py:253
  16.5 15.1 %collective-permute-start.3 = (bf16[1,88,768]{2,1,0:T(8,128)(2,1)S(1)}, bf16[1,88,768]{2,1,0:T(8,128)(2,1)S(1)}, u32[]{:S(2)}, u32[]{:S(2)}) collective-permute-start(bf16[1,88,768]{2,1,0:T(8,128)(2,1)S(1)} %dynamic-slice_bitcast_fusion.14), channel_id=1, source_target_pairs={{0,4},{1,5},{2,6},{3,7},{4,0},{5,1},{6,2},{7,3},{8,12},{9,13},{10,... | collective-permute-start | bytes 405512 | tf_op jit(solution)/shard_map/ppermute | solution.py:89
  22.8 38.1 %collective-permute-start.14 = (s32[2,10]{1,0:T(2,128)S(1)}, s32[2,10]{1,0:T(2,128)S(1)}, u32[]{:S(2)}, u32[]{:S(2)}) collective-permute-start(s32[2,10]{1,0:T(2,128)S(1)} %bitcast.575), channel_id=1, source_target_pairs={{0,2},{1,3},{2,0},{3,1},{4,6},{5,7},{6,4},{7,5},{8,10},{9,11},{10,... | collective-permute-start | bytes 248 | tf_op jit(solution)/shard_map/ppermute | solution.py:89
  41.3 17.8 %collective-permute-start.5 = (bf16[4,1,1,88,768]{4,3,0,2,1:T(8,128)(2,1)S(1)}, bf16[4,1,1,88,768]{4,3,0,2,1:T(8,128)(2,1)S(1)}, u32[]{:S(2)}, u32[]{:S(2)}) collective-permute-start(bf16[4,1,1,88,768]{4,3,0,2,1:T(8,128)(2,1)S(1)} %bitcast.548), channel_id=1, source_target_pairs={{0,16},{8,24},{16,0},{24,8},{1,17},{9,25},{17,1},{25,9},{2,18},{10... | collective-permute-start | bytes 1622024 | tf_op jit(solution)/shard_map/ppermute | solution.py:89
  42.9 18.5 %collective-permute-start.1 = (bf16[2,1312]{1,0:T(2,128)(2,1)S(1)}, bf16[2,1312]{1,0:T(2,128)(2,1)S(1)}, u32[]{:S(2)}, u32[]{:S(2)}) collective-permute-start(bf16[2,1312]{1,0:T(2,128)(2,1)S(1)} %maximum_bitcast_fusion.8), channel_id=1, source_target_pairs={{0,2},{1,3},{2,0},{3,1},{4,6},{5,7},{6,4},{7,5},{8,10},{9,11},{10,... | collective-permute-start | bytes 15752 | tf_op jit(solution)/shard_map/ppermute | solution.py:89
  49.5 16.3 %collective-permute-start.10 = (bf16[4,1,1,96,768]{4,3,0,2,1:T(8,128)(2,1)S(1)}, bf16[4,1,1,96,768]{4,3,0,2,1:T(8,128)(2,1)S(1)}, u32[]{:S(2)}, u32[]{:S(2)}) collective-permute-start(bf16[4,1,1,96,768]{4,3,0,2,1:T(8,128)(2,1)S(1)} %bitcast.537), channel_id=1, source_target_pairs={{0,1},{1,0},{2,3},{3,2},{4,5},{5,4},{6,7},{7,6},{8,9},{9,8},{10,11... | collective-permute-start | bytes 1769480 | tf_op jit(solution)/shard_map/ppermute | solution.py:89
  59.3 36.8 %collective-permute-start.6 = (bf16[4,1,2,88,768]{4,3,0,2,1:T(8,128)(2,1)S(1)}, bf16[4,1,2,88,768]{4,3,0,2,1:T(8,128)(2,1)S(1)}, u32[]{:S(2)}, u32[]{:S(2)}) collective-permute-start(bf16[4,1,2,88,768]{4,3,0,2,1:T(8,128)(2,1)S(1)} %maximum_bitcast_fusion.1), channel_id=1, source_target_pairs={{0,1},{1,0},{2,3},{3,2},{4,5},{5,4},{6,7},{7,6},{8,9},{9,8},{10,11... | collective-permute-start | bytes 3244040 | tf_op jit(solution)/shard_map/ppermute | solution.py:89
  66.0 38.1 %collective-permute-start.11 = (bf16[4,2,1,96,768]{4,3,0,1,2:T(8,128)(2,1)S(1)}, bf16[4,2,1,96,768]{4,3,0,1,2:T(8,128)(2,1)S(1)}, u32[]{:S(2)}, u32[]{:S(2)}) collective-permute-start(bf16[4,2,1,96,768]{4,3,0,1,2:T(8,128)(2,1)S(1)} %maximum_bitcast_fusion), channel_id=1, source_target_pairs={{0,16},{8,24},{16,0},{24,8},{1,17},{9,25},{17,1},{25,9},{2,18},{10... | collective-permute-start | bytes 3538952 | tf_op jit(solution)/shard_map/ppermute | solution.py:89
  102.6 121.4 %collective-permute-start.15 = (s32[4,10]{1,0:T(4,128)}, s32[4,10]{1,0:T(4,128)}, u32[]{:S(2)}, u32[]{:S(2)}) collective-permute-start(s32[4,10]{1,0:T(4,128)} %bitcast.62), channel_id=1, source_target_pairs={{0,4},{1,5},{2,6},{3,7},{4,0},{5,1},{6,2},{7,3},{8,12},{9,13},{10,... | collective-permute-start | bytes 488 | tf_op jit(solution)/shard_map/ppermute | solution.py:89
  106.0 26.7 %collective-permute-start.12 = (bf16[8,2,96,768]{3,2,0,1:T(8,128)(2,1)}, bf16[8,2,96,768]{3,2,0,1:T(8,128)(2,1)}, u32[]{:S(2)}, u32[]{:S(2)}) collective-permute-start(bf16[8,2,96,768]{3,2,0,1:T(8,128)(2,1)} %pad_maximum_fusion.2), channel_id=1, source_target_pairs={{0,8},{8,0},{16,24},{24,16},{1,9},{9,1},{17,25},{25,17},{2,10},{10... | collective-permute-start | bytes 7077896 | tf_op jit(solution)/shard_map/ppermute | solution.py:89
  284.3 31.7 %collective-permute-start.24 = (bf16[768,1792]{1,0:T(8,128)(2,1)}, bf16[768,1792]{1,0:T(8,128)(2,1)}, u32[]{:S(2)}, u32[]{:S(2)}) collective-permute-start(bf16[768,1792]{1,0:T(8,128)(2,1)} %pad_maximum_fusion.1), channel_id=1, source_target_pairs={{0,8},{8,0},{16,24},{24,16},{1,9},{9,1},{17,25},{25,17},{2,10},{10... | collective-permute-start | bytes 8257544 | tf_op jit(solution)/shard_map/ppermute | solution.py:89
  307.0 44.5 %collective-permute-start.25 = (bf16[2,2,2,192,384]{4,3,2,1,0:T(8,128)(2,1)}, bf16[2,2,2,192,384]{4,3,2,1,0:T(8,128)(2,1)}, u32[]{:S(2)}, u32[]{:S(2)}) collective-permute-start(bf16[2,2,2,192,384]{4,3,2,1,0:T(8,128)(2,1)} %dynamic-slice_bitcast_fusion.1), channel_id=1, source_target_pairs={{0,1},{1,0},{2,3},{3,2},{4,5},{5,4},{6,7},{7,6},{8,9},{9,8},{10,11... | collective-permute-start | bytes 3538952 | tf_op jit(solution)/shard_map/ppermute | solution.py:89
  340.1 32.1 %collective-permute-start.26 = (bf16[2,2,2,48,1792]{4,3,2,1,0:T(8,128)(2,1)}, bf16[2,2,2,48,1792]{4,3,2,1,0:T(8,128)(2,1)}, u32[]{:S(2)}, u32[]{:S(2)}) collective-permute-start(bf16[2,2,2,48,1792]{4,3,2,1,0:T(8,128)(2,1)} %dynamic-slice_bitcast_fusion), channel_id=1, source_target_pairs={{0,16},{8,24},{16,0},{24,8},{1,17},{9,25},{17,1},{25,9},{2,18},{10... | collective-permute-start | bytes 4128776 | tf_op jit(solution)/shard_map/ppermute | solution.py:89
  340.9 41.4 %collective-permute-start.27 = (bf16[1408,768]{0,1:T(8,128)(2,1)}, bf16[1408,768]{0,1:T(8,128)(2,1)}, u32[]{:S(2)}, u32[]{:S(2)}) collective-permute-start(bf16[1408,768]{0,1:T(8,128)(2,1)} %fusion.14), channel_id=1, source_target_pairs={{0,8},{8,0},{16,24},{24,16},{1,9},{9,1},{17,25},{25,17},{2,10},{10... | collective-permute-start | bytes 6488072 | tf_op jit(solution)/shard_map/ppermute | solution.py:89
  375.4 27.3 %collective-permute-start.28 = (bf16[2,2,192,384]{3,2,1,0:T(8,128)(2,1)}, bf16[2,2,192,384]{3,2,1,0:T(8,128)(2,1)}, u32[]{:S(2)}, u32[]{:S(2)}) collective-permute-start(bf16[2,2,192,384]{3,2,1,0:T(8,128)(2,1)} %dynamic-slice_bitcast_fusion.7), channel_id=1, source_target_pairs={{0,16},{8,24},{16,0},{24,8},{1,17},{9,25},{17,1},{25,9},{2,18},{10... | collective-permute-start | bytes 1769480 | tf_op jit(solution)/shard_map/ppermute | solution.py:89
  378.8 23.8 %collective-permute-start.29 = (bf16[2,2,48,1792]{3,2,1,0:T(8,128)(2,1)}, bf16[2,2,48,1792]{3,2,1,0:T(8,128)(2,1)}, u32[]{:S(2)}, u32[]{:S(2)}) collective-permute-start(bf16[2,2,48,1792]{3,2,1,0:T(8,128)(2,1)} %dynamic-slice_bitcast_fusion.6), channel_id=1, source_target_pairs={{0,1},{1,0},{2,3},{3,2},{4,5},{5,4},{6,7},{7,6},{8,9},{9,8},{10,11... | collective-permute-start | bytes 2064392 | tf_op jit(solution)/shard_map/ppermute | solution.py:89
  398.3 26.6 %collective-permute-start.31 = (bf16[2,2,2,88,768]{4,3,2,1,0:T(8,128)(2,1)}, bf16[2,2,2,88,768]{4,3,2,1,0:T(8,128)(2,1)}, u32[]{:S(2)}, u32[]{:S(2)}) collective-permute-start(bf16[2,2,2,88,768]{4,3,2,1,0:T(8,128)(2,1)} %dynamic-slice_bitcast_fusion.2), channel_id=1, source_target_pairs={{0,1},{1,0},{2,3},{3,2},{4,5},{5,4},{6,7},{7,6},{8,9},{9,8},{10,11... | collective-permute-start | bytes 3244040 | tf_op jit(solution)/shard_map/ppermute | solution.py:89
  409.5 26.0 %collective-permute-start.32 = (bf16[2,2,2,48,1152]{4,3,2,1,0:T(8,128)(2,1)}, bf16[2,2,2,48,1152]{4,3,2,1,0:T(8,128)(2,1)}, u32[]{:S(2)}, u32[]{:S(2)}) collective-permute-start(bf16[2,2,2,48,1152]{4,3,2,1,0:T(8,128)(2,1)} %dynamic-slice_bitcast_fusion.5), channel_id=1, source_target_pairs={{0,16},{8,24},{16,0},{24,8},{1,17},{9,25},{17,1},{25,9},{2,18},{10... | collective-permute-start | bytes 2654216 | tf_op jit(solution)/shard_map/ppermute | solution.py:89
  441.6 19.4 %collective-permute-start.33 = (bf16[768,1280]{0,1:T(8,128)(2,1)S(1)}, bf16[768,1280]{0,1:T(8,128)(2,1)S(1)}, u32[]{:S(2)}, u32[]{:S(2)}) collective-permute-start(bf16[768,1280]{0,1:T(8,128)(2,1)S(1)} %pad_maximum_fusion.5), channel_id=1, source_target_pairs={{0,8},{8,0},{16,24},{24,16},{1,9},{9,1},{17,25},{25,17},{2,10},{10... | collective-permute-start | bytes 5898248 | tf_op jit(solution)/shard_map/ppermute | solution.py:89
  468.6 24.7 %collective-permute-start.36 = (bf16[2,2,2,48,1280]{4,3,2,1,0:T(8,128)(2,1)}, bf16[2,2,2,48,1280]{4,3,2,1,0:T(8,128)(2,1)}, u32[]{:S(2)}, u32[]{:S(2)}) collective-permute-start(bf16[2,2,2,48,1280]{4,3,2,1,0:T(8,128)(2,1)} %dynamic-slice_bitcast_fusion.3), channel_id=1, source_target_pairs={{0,1},{1,0},{2,3},{3,2},{4,5},{5,4},{6,7},{7,6},{8,9},{9,8},{10,11... | collective-permute-start | bytes 2949128 | tf_op jit(solution)/shard_map/ppermute | solution.py:89
  472.0 21.3 %collective-permute-start.37 = (bf16[2,48,4864]{2,1,0:T(8,128)(2,1)}, bf16[2,48,4864]{2,1,0:T(8,128)(2,1)}, u32[]{:S(2)}, u32[]{:S(2)}) collective-permute-start(bf16[2,48,4864]{2,1,0:T(8,128)(2,1)} %dynamic-slice_bitcast_fusion.4), channel_id=1, source_target_pairs={{0,2},{1,3},{2,0},{3,1},{4,6},{5,7},{6,4},{7,5},{8,10},{9,11},{10,... | collective-permute-start | bytes 2801672 | tf_op jit(solution)/shard_map/ppermute | solution.py:89
  494.8 23.7 %collective-permute-start.38 = (bf16[2,2,48,1280]{3,2,1,0:T(8,128)(2,1)S(1)}, bf16[2,2,48,1280]{3,2,1,0:T(8,128)(2,1)S(1)}, u32[]{:S(2)}, u32[]{:S(2)}) collective-permute-start(bf16[2,2,48,1280]{3,2,1,0:T(8,128)(2,1)S(1)} %dynamic-slice_bitcast_fusion.9), channel_id=1, source_target_pairs={{0,16},{8,24},{16,0},{24,8},{1,17},{9,25},{17,1},{25,9},{2,18},{10... | collective-permute-start | bytes 1474568 | tf_op jit(solution)/shard_map/ppermute | solution.py:89
  497.5 21.0 %collective-permute-start.39 = (bf16[48,4864]{1,0:T(8,128)(2,1)S(1)}, bf16[48,4864]{1,0:T(8,128)(2,1)S(1)}, u32[]{:S(2)}, u32[]{:S(2)}) collective-permute-start(bf16[48,4864]{1,0:T(8,128)(2,1)S(1)} %dynamic-slice_bitcast_fusion.10), channel_id=1, source_target_pairs={{0,4},{1,5},{2,6},{3,7},{4,0},{5,1},{6,2},{7,3},{8,12},{9,13},{10,... | collective-permute-start | bytes 1400840 | tf_op jit(solution)/shard_map/ppermute | solution.py:89
  (165 other events, 1305.3 us)
Sparse Core Ops, SparseCore 0:
  11.7 80.6 all-gather.2
  95.8 73.7 all-gather.4
